TPU v7x, 32 devices: a whole 2x2x4 slice. The times are simulated.
32 devices in a mesh: row: 8 (over z, x), col: 4 (over y, core).
Axes of the slice: x: 2, y: 2, z: 4, core: 2. Of those that a mesh axis runs over, the one named last changes fastest.
Arguments:
- margin: bfloat16 [32, 128, 1152], P(('row', 'col')), may hold values from -0.2 to 1.2, as said below
- fock_matrix: bfloat16 [32, 128, 1152], P(('row', 'col')), may hold values from -0.4 to 0.4, as said below
- density: bfloat16 [32, 128, 1152], P(('row', 'col')), may hold values from -4 to 4, as said below
- present: int32 [32, 9], P(('row', 'col')), may hold values from 0 to 1, as said below
Outputs:
- gradient: float32 [32, 128, 1152], P(('row', 'col'))
- updated: float32 [32, 128, 1152], P(('row', 'col'))
Inputs may be any that keep to these rules, and one draw needn't show every extreme that they name: present[r, 4] is 1; present[r, o + 4] equals present[r + o, 4 - o]; slots whose block lies outside the matrix are 0. `margin`: symmetric: block (r, o) is the transpose of block (r + o, -o); blocks where present is 0 are zero. `fock_matrix`: symmetric: block (r, o) is the transpose of block (r + o, -o); blocks where present is 0 are zero. `density`: symmetric: block (r, o) is the transpose of block (r + o, -o); blocks where present is 0 are zero.
All inputs are finite; a program needn't handle non-finite values.
Results may differ from a plain program's by a relative error of at most 0.0041.
Values may be sent and summed in bfloat16 or wider, within the bound.
A program may use at most 64 MiB of HBM per device.

v0:
```python
import jax
import jax.numpy as jnp
from jax import lax
from jax.sharding import PartitionSpec as P

HALF_BAND = 4


step_scale = 0.015625


def shifted(value, axis, steps):
    count = lax.axis_size(axis)
    initial, last = (max(0, -steps), min(count, count - steps))
    return lax.ppermute(value, axis, [(source, source + steps) for source in range(initial, last)])


def band_product(left_band, right_wide, present):
    row_count = left_band.shape[0]
    block_size = left_band.shape[1]
    band_count = present.shape[1]
    half_band = (band_count - 1) // 2
    left_blocks = left_band.reshape(row_count, block_size, band_count, block_size)
    right_blocks = right_wide.reshape(right_wide.shape[0], block_size, band_count, block_size)
    accumulated = jnp.zeros((row_count, block_size, band_count, block_size), jnp.float32)
    for p in range(band_count):
        first_col = max(0, half_band - p)
        last_col = min(band_count, band_count + half_band - p)
        contribution = jnp.einsum(
            "rik,rkqc->riqc",
            left_blocks[:, :, p, :],
            right_blocks[p : p + row_count, :, first_col:last_col, :],
            preferred_element_type=jnp.float32,
        )
        accumulated = accumulated + jnp.pad(
            contribution,
            (
                (0, 0),
                (0, 0),
                (first_col + p - half_band, band_count - (last_col + p - half_band)),
                (0, 0),
            ),
        )
    keep_mask = present.astype(jnp.float32)[:, None, :, None]
    return (accumulated * keep_mask).reshape(row_count, block_size, band_count * block_size)


def extend(local_rows, reach_rows, sender):
    row_count = local_rows.shape[0]
    reach_count = -(-reach_rows // row_count)
    below = [sender(local_rows, k) for k in range(reach_count, 0, -1)]
    above = [sender(local_rows, -k) for k in range(1, reach_count + 1)]
    joined = jnp.concatenate(below + [local_rows] + above, axis=0)
    first_row = reach_count * row_count - reach_rows
    return joined


def rows_ahead(slab, distance):
    row_count = slab.shape[0]
    device_step = distance // row_count
    remainder = distance % row_count
    wanted = [device_step]
    pieces = []
    for device_offset in wanted:
        if device_offset == 0:
            pieces.append(slab)
        else:
            pieces.append(shifted(slab, ("row", "col"), -device_offset))
    joined = pieces[0]
    return joined


def mirror_of(band, band_count):
    half_band = (band_count - 1) // 2
    row_count = band.shape[0]
    block_size = band.shape[1]
    blocks = band.reshape(row_count, block_size, band_count, block_size)
    slot_list = []
    for distance in range(-half_band, half_band + 1):
        slab = blocks[:, :, half_band - distance, :]
        slot_list.append(jnp.swapaxes(rows_ahead(slab, distance), 1, 2))
    return jnp.stack(slot_list, axis=2).reshape(row_count, block_size, band_count * block_size)


def local(margin, fock_matrix, density, present):
    band_count = present.shape[1]
    half_band = HALF_BAND
    margin_wide = extend(
        margin, half_band, lambda block_rows, offset: shifted(block_rows, ("row", "col"), offset)
    )
    dens_over = band_product(density, margin_wide, present).astype(jnp.bfloat16)
    dens_wide = extend(
        dens_over, half_band, lambda block_rows, offset: shifted(block_rows, ("row", "col"), offset)
    )
    fock_dens = band_product(fock_matrix, dens_wide, present).astype(jnp.bfloat16)
    gradient = fock_dens.astype(jnp.float32) - mirror_of(fock_dens, band_count).astype(jnp.float32)
    step_matrix = (-step_scale * gradient).astype(jnp.bfloat16)
    step_wide = extend(
        step_matrix,
        half_band,
        lambda block_rows, offset: shifted(block_rows, ("row", "col"), offset),
    )
    first_term = band_product(dens_over, step_wide, present).astype(jnp.bfloat16)
    commuted = first_term.astype(jnp.float32) + mirror_of(first_term, band_count).astype(
        jnp.float32
    )
    commuted_half = commuted.astype(jnp.bfloat16)
    comm_over = band_product(commuted_half, margin_wide, present).astype(jnp.bfloat16)
    second_term = band_product(comm_over, step_wide, present).astype(jnp.bfloat16)
    second_mirror = mirror_of(second_term, band_count).astype(jnp.float32)
    updated = (
        density.astype(jnp.float32)
        + commuted
        + 0.5 * (second_term.astype(jnp.float32) + second_mirror)
    )
    return (gradient, updated)


def solution(mesh):
    in_specs = (
        P(("row", "col"), None, None),
        P(("row", "col"), None, None),
        P(("row", "col"), None, None),
        P(("row", "col"), None),
    )
    out_specs = (P(("row", "col"), None, None), P(("row", "col"), None, None))
    return jax.shard_map(local, mesh=mesh, in_specs=in_specs, out_specs=out_specs, check_vma=False)
```

profile of v0, /device:TPU:10, one launch (start us, length us, event | category | flops | bytes accessed | tf_op | source)
XLA Modules:
  0.0 238.6 jit_solution(11204142905765786402)
XLA Ops:
  0.6 3.6 %collective-permute-start = (bf16[1,128,1152]{2,1,0:T(8,128)(2,1)}, bf16[1,128,1152]{2,1,0:T(8,128)(2,1)S(1)}, u32[]{:S(2)}, u32[]{:S(2)}) collective-permute-start(bf16[1,128,1152]{2,1,0:T(8,128)(2,1)} %param.4), channel_id=1, source_target_pairs={{0,4},{1,5},{2,6},{3,7},{4,8},{5,9},{6,10},{7,11},{8,12},{9,13},{1... | collective-permute-start | bytes 884744 | tf_op jit(solution)/shard_map/ppermute | solution.py:15
  4.2 2.6 %collective-permute-start.1 = (bf16[1,128,1152]{2,1,0:T(8,128)(2,1)}, bf16[1,128,1152]{2,1,0:T(8,128)(2,1)S(1)}, u32[]{:S(2)}, u32[]{:S(2)}) collective-permute-start(bf16[1,128,1152]{2,1,0:T(8,128)(2,1)} %param.4), channel_id=1, source_target_pairs={{0,3},{1,4},{2,5},{3,6},{4,7},{5,8},{6,9},{7,10},{8,11},{9,12},{10... | collective-permute-start | bytes 884744 | tf_op jit(solution)/shard_map/ppermute | solution.py:15
  6.8 3.3 %collective-permute-start.2 = (bf16[1,128,1152]{2,1,0:T(8,128)(2,1)}, bf16[1,128,1152]{2,1,0:T(8,128)(2,1)S(1)}, u32[]{:S(2)}, u32[]{:S(2)}) collective-permute-start(bf16[1,128,1152]{2,1,0:T(8,128)(2,1)} %param.4), channel_id=1, source_target_pairs={{0,2},{1,3},{2,4},{3,5},{4,6},{5,7},{6,8},{7,9},{8,10},{9,11},{10,... | collective-permute-start | bytes 884744 | tf_op jit(solution)/shard_map/ppermute | solution.py:15
  10.2 2.6 %collective-permute-start.3 = (bf16[1,128,1152]{2,1,0:T(8,128)(2,1)}, bf16[1,128,1152]{2,1,0:T(8,128)(2,1)S(1)}, u32[]{:S(2)}, u32[]{:S(2)}) collective-permute-start(bf16[1,128,1152]{2,1,0:T(8,128)(2,1)} %param.4), channel_id=1, source_target_pairs={{0,1},{1,2},{2,3},{3,4},{4,5},{5,6},{6,7},{7,8},{8,9},{9,10},{10,1... | collective-permute-start | bytes 884744 | tf_op jit(solution)/shard_map/ppermute | solution.py:15
  12.8 3.8 %collective-permute-start.4 = (bf16[1,128,1152]{2,1,0:T(8,128)(2,1)}, bf16[1,128,1152]{2,1,0:T(8,128)(2,1)S(1)}, u32[]{:S(2)}, u32[]{:S(2)}) collective-permute-start(bf16[1,128,1152]{2,1,0:T(8,128)(2,1)} %param.4), channel_id=1, source_target_pairs={{1,0},{2,1},{3,2},{4,3},{5,4},{6,5},{7,6},{8,7},{9,8},{10,9},{11,1... | collective-permute-start | bytes 884744 | tf_op jit(solution)/shard_map/ppermute | solution.py:15
  17.8 1.4 fusion.11
  19.9 2.5 %collective-permute-start.5 = (bf16[1,128,1152]{2,1,0:T(8,128)(2,1)}, bf16[1,128,1152]{2,1,0:T(8,128)(2,1)S(1)}, u32[]{:S(2)}, u32[]{:S(2)}) collective-permute-start(bf16[1,128,1152]{2,1,0:T(8,128)(2,1)} %param.4), channel_id=1, source_target_pairs={{2,0},{3,1},{4,2},{5,3},{6,4},{7,5},{8,6},{9,7},{10,8},{11,9},{12,... | collective-permute-start | bytes 884744 | tf_op jit(solution)/shard_map/ppermute | solution.py:15
  23.1 2.5 %collective-permute-start.6 = (bf16[1,128,1152]{2,1,0:T(8,128)(2,1)}, bf16[1,128,1152]{2,1,0:T(8,128)(2,1)S(1)}, u32[]{:S(2)}, u32[]{:S(2)}) collective-permute-start(bf16[1,128,1152]{2,1,0:T(8,128)(2,1)} %param.4), channel_id=1, source_target_pairs={{3,0},{4,1},{5,2},{6,3},{7,4},{8,5},{9,6},{10,7},{11,8},{12,9},{13... | collective-permute-start | bytes 884744 | tf_op jit(solution)/shard_map/ppermute | solution.py:15
  26.5 3.3 %collective-permute-start.7 = (bf16[1,128,1152]{2,1,0:T(8,128)(2,1)S(1)}, bf16[1,128,1152]{2,1,0:T(8,128)(2,1)S(1)}, u32[]{:S(2)}, u32[]{:S(2)}) collective-permute-start(bf16[1,128,1152]{2,1,0:T(8,128)(2,1)S(1)} %copy-done.6), channel_id=1, source_target_pairs={{4,0},{5,1},{6,2},{7,3},{8,4},{9,5},{10,6},{11,7},{12,8},{13,9},{1... | collective-permute-start | bytes 884744 | tf_op jit(solution)/shard_map/ppermute | solution.py:15
  32.7 8.2 %collective-permute-done.5 = bf16[1,128,1152]{2,1,0:T(8,128)(2,1)S(1)} collective-permute-done((bf16[1,128,1152]{2,1,0:T(8,128)(2,1)}, bf16[1,128,1152]{2,1,0:T(8,128)(2,1)S(1)}, u32[]{:S(2)}, u32[]{:S(2)}) %collective-permute-start.5) | collective-permute-done | bytes 294944 | tf_op jit(solution)/shard_map/ppermute | solution.py:15
  42.4 1.9 collective-permute-done.7
  45.1 4.5 %copy.65 = bf16[9,128,1152]{1,2,0:T(8,128)(2,1)S(1)} copy(bf16[9,128,1152]{2,1,0:T(8,128)(2,1)} %constant_dynamic-update-slice_fusion) | data formatting | bytes 5308416 | tf_op jit(solution)/shard_map/concatenate | solution.py:53
  51.6 1.9 collective-permute-start.13
  53.5 3.9 %collective-permute-start.10 = (bf16[1,128,1152]{1,2,0:T(8,128)(2,1)S(1)}, bf16[1,128,1152]{1,2,0:T(8,128)(2,1)}, u32[]{:S(2)}, u32[]{:S(2)}) collective-permute-start(bf16[1,128,1152]{1,2,0:T(8,128)(2,1)S(1)} %bitcast.726), channel_id=1, source_target_pairs={{0,2},{1,3},{2,4},{3,5},{4,6},{5,7},{6,8},{7,9},{8,10},{9,11},{10,... | collective-permute-start | bytes 884744 | tf_op jit(solution)/shard_map/ppermute | solution.py:15
  57.4 1.9 collective-permute-start.14
  60.5 2.7 %collective-permute-start.12 = (bf16[1,128,1152]{1,2,0:T(8,128)(2,1)S(1)}, bf16[1,128,1152]{1,2,0:T(8,128)(2,1)S(1)}, u32[]{:S(2)}, u32[]{:S(2)}) collective-permute-start(bf16[1,128,1152]{1,2,0:T(8,128)(2,1)S(1)} %bitcast.728), channel_id=1, source_target_pairs={{1,0},{2,1},{3,2},{4,3},{5,4},{6,5},{7,6},{8,7},{9,8},{10,9},{11,1... | collective-permute-start | bytes 884744 | tf_op jit(solution)/shard_map/ppermute | solution.py:15
  63.2 2.1 collective-permute-start.11
  65.4 7.5 %collective-permute-done.13 = bf16[1,128,1152]{1,2,0:T(8,128)(2,1)} collective-permute-done((bf16[1,128,1152]{1,2,0:T(8,128)(2,1)S(1)}, bf16[1,128,1152]{1,2,0:T(8,128)(2,1)}, u32[]{:S(2)}, u32[]{:S(2)}) %collective-permute-start.13) | collective-permute-done | bytes 294944 | tf_op jit(solution)/shard_map/ppermute | solution.py:15
  72.9 1.9 collective-permute-start.9
  76.0 1.9 collective-permute-start.15
  79.1 4.8 %collective-permute-start.8 = (bf16[1,128,1152]{1,2,0:T(8,128)(2,1)S(1)}, bf16[1,128,1152]{1,2,0:T(8,128)(2,1)S(1)}, u32[]{:S(2)}, u32[]{:S(2)}) collective-permute-start(bf16[1,128,1152]{1,2,0:T(8,128)(2,1)S(1)} %bitcast.732), channel_id=1, source_target_pairs={{0,4},{1,5},{2,6},{3,7},{4,8},{5,9},{6,10},{7,11},{8,12},{9,13},{1... | collective-permute-start | bytes 884744 | tf_op jit(solution)/shard_map/ppermute | solution.py:15
  85.0 4.0 %collective-permute-done.9 = bf16[1,128,1152]{1,2,0:T(8,128)(2,1)S(1)} collective-permute-done((bf16[1,128,1152]{1,2,0:T(8,128)(2,1)S(1)}, bf16[1,128,1152]{1,2,0:T(8,128)(2,1)S(1)}, u32[]{:S(2)}, u32[]{:S(2)}) %collective-permute-start.9) | collective-permute-done | bytes 294944 | tf_op jit(solution)/shard_map/ppermute | solution.py:15
  93.0 3.0 %collective-permute-start.16 = (bf16[1,128,128]{1,2,0:T(8,128)(2,1)S(1)}, bf16[1,128,128]{1,2,0:T(8,128)(2,1)S(1)}, u32[]{:S(2)}, u32[]{:S(2)}) collective-permute-start(bf16[1,128,128]{1,2,0:T(8,128)(2,1)S(1)} %get-tuple-element.29), channel_id=1, source_target_pairs={{0,4},{1,5},{2,6},{3,7},{4,8},{5,9},{6,10},{7,11},{8,12},{9,13},{1... | collective-permute-start | bytes 98312 | tf_op jit(solution)/shard_map/ppermute | solution.py:15
  96.2 4.9 %collective-permute-start.17 = (bf16[1,128,128]{1,2,0:T(8,128)(2,1)}, bf16[1,128,128]{1,2,0:T(8,128)(2,1)S(1)}, u32[]{:S(2)}, u32[]{:S(2)}) collective-permute-start(bf16[1,128,128]{1,2,0:T(8,128)(2,1)} %get-tuple-element.28), channel_id=1, source_target_pairs={{0,3},{1,4},{2,5},{3,6},{4,7},{5,8},{6,9},{7,10},{8,11},{9,12},{10... | collective-permute-start | bytes 98312 | tf_op jit(solution)/shard_map/ppermute | solution.py:15
  101.1 2.6 %collective-permute-start.18 = (bf16[1,128,128]{1,2,0:T(8,128)(2,1)}, bf16[1,128,128]{1,2,0:T(8,128)(2,1)S(1)}, u32[]{:S(2)}, u32[]{:S(2)}) collective-permute-start(bf16[1,128,128]{1,2,0:T(8,128)(2,1)} %get-tuple-element.27), channel_id=1, source_target_pairs={{0,2},{1,3},{2,4},{3,5},{4,6},{5,7},{6,8},{7,9},{8,10},{9,11},{10,... | collective-permute-start | bytes 98312 | tf_op jit(solution)/shard_map/ppermute | solution.py:15
  103.7 1.9 collective-permute-start.19
  105.6 4.5 %collective-permute-start.20 = (bf16[1,128,128]{1,2,0:T(8,128)(2,1)}, bf16[1,128,128]{1,2,0:T(8,128)(2,1)S(1)}, u32[]{:S(2)}, u32[]{:S(2)}) collective-permute-start(bf16[1,128,128]{1,2,0:T(8,128)(2,1)} %get-tuple-element.25), channel_id=1, source_target_pairs={{1,0},{2,1},{3,2},{4,3},{5,4},{6,5},{7,6},{8,7},{9,8},{10,9},{11,1... | collective-permute-start | bytes 98312 | tf_op jit(solution)/shard_map/ppermute | solution.py:15
  110.8 3.3 %collective-permute-start.21 = (bf16[1,128,128]{1,2,0:T(8,128)(2,1)}, bf16[1,128,128]{1,2,0:T(8,128)(2,1)S(1)}, u32[]{:S(2)}, u32[]{:S(2)}) collective-permute-start(bf16[1,128,128]{1,2,0:T(8,128)(2,1)} %get-tuple-element.24), channel_id=1, source_target_pairs={{2,0},{3,1},{4,2},{5,3},{6,4},{7,5},{8,6},{9,7},{10,8},{11,9},{12,... | collective-permute-start | bytes 98312 | tf_op jit(solution)/shard_map/ppermute | solution.py:15
  114.8 1.9 collective-permute-start.22
  116.8 2.8 %collective-permute-start.23 = (bf16[1,128,128]{1,2,0:T(8,128)(2,1)}, bf16[1,128,128]{1,2,0:T(8,128)(2,1)S(1)}, u32[]{:S(2)}, u32[]{:S(2)}) collective-permute-start(bf16[1,128,128]{1,2,0:T(8,128)(2,1)} %get-tuple-element.22), channel_id=1, source_target_pairs={{4,0},{5,1},{6,2},{7,3},{8,4},{9,5},{10,6},{11,7},{12,8},{13,9},{1... | collective-permute-start | bytes 98312 | tf_op jit(solution)/shard_map/ppermute | solution.py:15
  120.3 3.7 %collective-permute-done.23 = bf16[1,128,128]{1,2,0:T(8,128)(2,1)S(1)} collective-permute-done((bf16[1,128,128]{1,2,0:T(8,128)(2,1)}, bf16[1,128,128]{1,2,0:T(8,128)(2,1)S(1)}, u32[]{:S(2)}, u32[]{:S(2)}) %collective-permute-start.23) | collective-permute-done | bytes 32800 | tf_op jit(solution)/shard_map/ppermute | solution.py:15
  125.6 1.3 copy.88
  126.9 2.4 %collective-permute-start.26 = (bf16[1,128,1152]{1,2,0:T(8,128)(2,1)S(1)}, bf16[1,128,1152]{1,2,0:T(8,128)(2,1)S(1)}, u32[]{:S(2)}, u32[]{:S(2)}) collective-permute-start(bf16[1,128,1152]{1,2,0:T(8,128)(2,1)S(1)} %multiply_convert_fusion.3), channel_id=1, source_target_pairs={{0,2},{1,3},{2,4},{3,5},{4,6},{5,7},{6,8},{7,9},{8,10},{9,11},{10,... | collective-permute-start | bytes 884744 | tf_op jit(solution)/shard_map/ppermute | solution.py:15
  129.4 4.4 %collective-permute-start.29 = (bf16[1,128,1152]{1,2,0:T(8,128)(2,1)S(1)}, bf16[1,128,1152]{1,2,0:T(8,128)(2,1)S(1)}, u32[]{:S(2)}, u32[]{:S(2)}) collective-permute-start(bf16[1,128,1152]{1,2,0:T(8,128)(2,1)S(1)} %multiply_convert_fusion.3), channel_id=1, source_target_pairs={{2,0},{3,1},{4,2},{5,3},{6,4},{7,5},{8,6},{9,7},{10,8},{11,9},{12,... | collective-permute-start | bytes 884744 | tf_op jit(solution)/shard_map/ppermute | solution.py:15
  133.8 1.9 collective-permute-start.25
  135.8 2.9 %collective-permute-start.24 = (bf16[1,128,1152]{1,2,0:T(8,128)(2,1)S(1)}, bf16[1,128,1152]{1,2,0:T(8,128)(2,1)S(1)}, u32[]{:S(2)}, u32[]{:S(2)}) collective-permute-start(bf16[1,128,1152]{1,2,0:T(8,128)(2,1)S(1)} %multiply_convert_fusion.3), channel_id=1, source_target_pairs={{0,4},{1,5},{2,6},{3,7},{4,8},{5,9},{6,10},{7,11},{8,12},{9,13},{1... | collective-permute-start | bytes 884744 | tf_op jit(solution)/shard_map/ppermute | solution.py:15
  138.7 3.0 %collective-permute-start.27 = (bf16[1,128,1152]{1,2,0:T(8,128)(2,1)S(1)}, bf16[1,128,1152]{1,2,0:T(8,128)(2,1)S(1)}, u32[]{:S(2)}, u32[]{:S(2)}) collective-permute-start(bf16[1,128,1152]{1,2,0:T(8,128)(2,1)S(1)} %multiply_convert_fusion.3), channel_id=1, source_target_pairs={{0,1},{1,2},{2,3},{3,4},{4,5},{5,6},{6,7},{7,8},{8,9},{9,10},{10,1... | collective-permute-start | bytes 884744 | tf_op jit(solution)/shard_map/ppermute | solution.py:15
  142.4 3.0 %collective-permute-start.30 = (bf16[1,128,1152]{1,2,0:T(8,128)(2,1)S(1)}, bf16[1,128,1152]{1,2,0:T(8,128)(2,1)S(1)}, u32[]{:S(2)}, u32[]{:S(2)}) collective-permute-start(bf16[1,128,1152]{1,2,0:T(8,128)(2,1)S(1)} %multiply_convert_fusion.3), channel_id=1, source_target_pairs={{3,0},{4,1},{5,2},{6,3},{7,4},{8,5},{9,6},{10,7},{11,8},{12,9},{13... | collective-permute-start | bytes 884744 | tf_op jit(solution)/shard_map/ppermute | solution.py:15
  146.5 4.2 %collective-permute-done.29 = bf16[1,128,1152]{1,2,0:T(8,128)(2,1)S(1)} collective-permute-done((bf16[1,128,1152]{1,2,0:T(8,128)(2,1)S(1)}, bf16[1,128,1152]{1,2,0:T(8,128)(2,1)S(1)}, u32[]{:S(2)}, u32[]{:S(2)}) %collective-permute-start.29) | collective-permute-done | bytes 294944 | tf_op jit(solution)/shard_map/ppermute | solution.py:15
  150.7 2.8 %collective-permute-start.28 = (bf16[1,128,1152]{1,2,0:T(8,128)(2,1)S(1)}, bf16[1,128,1152]{1,2,0:T(8,128)(2,1)S(1)}, u32[]{:S(2)}, u32[]{:S(2)}) collective-permute-start(bf16[1,128,1152]{1,2,0:T(8,128)(2,1)S(1)} %multiply_convert_fusion.3), channel_id=1, source_target_pairs={{1,0},{2,1},{3,2},{4,3},{5,4},{6,5},{7,6},{8,7},{9,8},{10,9},{11,1... | collective-permute-start | bytes 884744 | tf_op jit(solution)/shard_map/ppermute | solution.py:15
  154.5 3.4 %collective-permute-done.25 = bf16[1,128,1152]{1,2,0:T(8,128)(2,1)S(1)} collective-permute-done((bf16[1,128,1152]{1,2,0:T(8,128)(2,1)S(1)}, bf16[1,128,1152]{1,2,0:T(8,128)(2,1)S(1)}, u32[]{:S(2)}, u32[]{:S(2)}) %collective-permute-start.25) | collective-permute-done | bytes 294944 | tf_op jit(solution)/shard_map/ppermute | solution.py:15
  157.9 1.9 collective-permute-start.31
  162.0 5.4 %collective-permute-done.31 = bf16[1,128,1152]{1,2,0:T(8,128)(2,1)S(1)} collective-permute-done((bf16[1,128,1152]{1,2,0:T(8,128)(2,1)S(1)}, bf16[1,128,1152]{1,2,0:T(8,128)(2,1)S(1)}, u32[]{:S(2)}, u32[]{:S(2)}) %collective-permute-start.31) | collective-permute-done | bytes 294944 | tf_op jit(solution)/shard_map/ppermute | solution.py:15
  170.1 3.1 %collective-permute-start.32 = (bf16[1,128,128]{1,2,0:T(8,128)(2,1)}, bf16[1,128,128]{1,2,0:T(8,128)(2,1)}, u32[]{:S(2)}, u32[]{:S(2)}) collective-permute-start(bf16[1,128,128]{1,2,0:T(8,128)(2,1)} %get-tuple-element.21), channel_id=1, source_target_pairs={{0,4},{1,5},{2,6},{3,7},{4,8},{5,9},{6,10},{7,11},{8,12},{9,13},{1... | collective-permute-start | bytes 98312 | tf_op jit(solution)/shard_map/ppermute | solution.py:15
  173.2 1.8 copy.72
  175.0 1.8 copy.116
  176.9 1.9 collective-permute-start.33
  178.8 2.4 collective-permute-start.34
  181.2 2.9 %collective-permute-start.35 = (bf16[1,128,128]{1,2,0:T(8,128)(2,1)}, bf16[1,128,128]{1,2,0:T(8,128)(2,1)S(1)}, u32[]{:S(2)}, u32[]{:S(2)}) collective-permute-start(bf16[1,128,128]{1,2,0:T(8,128)(2,1)} %get-tuple-element.18), channel_id=1, source_target_pairs={{0,1},{1,2},{2,3},{3,4},{4,5},{5,6},{6,7},{7,8},{8,9},{9,10},{10,1... | collective-permute-start | bytes 98312 | tf_op jit(solution)/shard_map/ppermute | solution.py:15
  184.0 4.2 %collective-permute-start.36 = (bf16[1,128,128]{1,2,0:T(8,128)(2,1)}, bf16[1,128,128]{1,2,0:T(8,128)(2,1)S(1)}, u32[]{:S(2)}, u32[]{:S(2)}) collective-permute-start(bf16[1,128,128]{1,2,0:T(8,128)(2,1)} %get-tuple-element.17), channel_id=1, source_target_pairs={{1,0},{2,1},{3,2},{4,3},{5,4},{6,5},{7,6},{8,7},{9,8},{10,9},{11,1... | collective-permute-start | bytes 98312 | tf_op jit(solution)/shard_map/ppermute | solution.py:15
  188.2 2.9 %collective-permute-start.37 = (bf16[1,128,128]{1,2,0:T(8,128)(2,1)}, bf16[1,128,128]{1,2,0:T(8,128)(2,1)S(1)}, u32[]{:S(2)}, u32[]{:S(2)}) collective-permute-start(bf16[1,128,128]{1,2,0:T(8,128)(2,1)} %get-tuple-element.16), channel_id=1, source_target_pairs={{2,0},{3,1},{4,2},{5,3},{6,4},{7,5},{8,6},{9,7},{10,8},{11,9},{12,... | collective-permute-start | bytes 98312 | tf_op jit(solution)/shard_map/ppermute | solution.py:15
  191.9 3.2 %collective-permute-start.38 = (bf16[1,128,128]{1,2,0:T(8,128)(2,1)}, bf16[1,128,128]{1,2,0:T(8,128)(2,1)S(1)}, u32[]{:S(2)}, u32[]{:S(2)}) collective-permute-start(bf16[1,128,128]{1,2,0:T(8,128)(2,1)} %get-tuple-element.15), channel_id=1, source_target_pairs={{3,0},{4,1},{5,2},{6,3},{7,4},{8,5},{9,6},{10,7},{11,8},{12,9},{13... | collective-permute-start | bytes 98312 | tf_op jit(solution)/shard_map/ppermute | solution.py:15
  195.1 3.6 %collective-permute-start.39 = (bf16[1,128,128]{1,2,0:T(8,128)(2,1)}, bf16[1,128,128]{1,2,0:T(8,128)(2,1)S(1)}, u32[]{:S(2)}, u32[]{:S(2)}) collective-permute-start(bf16[1,128,128]{1,2,0:T(8,128)(2,1)} %get-tuple-element.14), channel_id=1, source_target_pairs={{4,0},{5,1},{6,2},{7,3},{8,4},{9,5},{10,6},{11,7},{12,8},{13,9},{1... | collective-permute-start | bytes 98312 | tf_op jit(solution)/shard_map/ppermute | solution.py:15
  199.6 2.4 %collective-permute-done.39 = bf16[1,128,128]{1,2,0:T(8,128)(2,1)S(1)} collective-permute-done((bf16[1,128,128]{1,2,0:T(8,128)(2,1)}, bf16[1,128,128]{1,2,0:T(8,128)(2,1)S(1)}, u32[]{:S(2)}, u32[]{:S(2)}) %collective-permute-start.39) | collective-permute-done | bytes 32800 | tf_op jit(solution)/shard_map/ppermute | solution.py:15
  202.0 1.9 convert_add_fusion
  208.3 2.0 collective-permute-start.40
  211.6 2.2 collective-permute-start.41
  213.8 3.7 %collective-permute-start.42 = (bf16[1,128,128]{1,2,0:T(8,128)(2,1)S(1)}, bf16[1,128,128]{1,2,0:T(8,128)(2,1)S(1)}, u32[]{:S(2)}, u32[]{:S(2)}) collective-permute-start(bf16[1,128,128]{1,2,0:T(8,128)(2,1)S(1)} %get-tuple-element.11), channel_id=1, source_target_pairs={{0,2},{1,3},{2,4},{3,5},{4,6},{5,7},{6,8},{7,9},{8,10},{9,11},{10,... | collective-permute-start | bytes 98312 | tf_op jit(solution)/shard_map/ppermute | solution.py:15
  217.5 1.9 collective-permute-start.43
  219.4 4.5 %collective-permute-start.44 = (bf16[1,128,128]{1,2,0:T(8,128)(2,1)S(1)}, bf16[1,128,128]{1,2,0:T(8,128)(2,1)S(1)}, u32[]{:S(2)}, u32[]{:S(2)}) collective-permute-start(bf16[1,128,128]{1,2,0:T(8,128)(2,1)S(1)} %get-tuple-element.9), channel_id=1, source_target_pairs={{1,0},{2,1},{3,2},{4,3},{5,4},{6,5},{7,6},{8,7},{9,8},{10,9},{11,1... | collective-permute-start | bytes 98312 | tf_op jit(solution)/shard_map/ppermute | solution.py:15
  224.2 2.1 collective-permute-start.45
  226.4 4.0 %collective-permute-start.46 = (bf16[1,128,128]{1,2,0:T(8,128)(2,1)S(1)}, bf16[1,128,128]{1,2,0:T(8,128)(2,1)S(1)}, u32[]{:S(2)}, u32[]{:S(2)}) collective-permute-start(bf16[1,128,128]{1,2,0:T(8,128)(2,1)S(1)} %get-tuple-element.7), channel_id=1, source_target_pairs={{3,0},{4,1},{5,2},{6,3},{7,4},{8,5},{9,6},{10,7},{11,8},{12,9},{13... | collective-permute-start | bytes 98312 | tf_op jit(solution)/shard_map/ppermute | solution.py:15
  230.4 3.6 %collective-permute-start.47 = (bf16[1,128,128]{1,2,0:T(8,128)(2,1)S(1)}, bf16[1,128,128]{1,2,0:T(8,128)(2,1)S(1)}, u32[]{:S(2)}, u32[]{:S(2)}) collective-permute-start(bf16[1,128,128]{1,2,0:T(8,128)(2,1)S(1)} %get-tuple-element.6), channel_id=1, source_target_pairs={{4,0},{5,1},{6,2},{7,3},{8,4},{9,5},{10,6},{11,7},{12,8},{13,9},{1... | collective-permute-start | bytes 98312 | tf_op jit(solution)/shard_map/ppermute | solution.py:15
  234.2 2.9 %collective-permute-done.47 = bf16[1,128,128]{1,2,0:T(8,128)(2,1)S(1)} collective-permute-done((bf16[1,128,128]{1,2,0:T(8,128)(2,1)S(1)}, bf16[1,128,128]{1,2,0:T(8,128)(2,1)S(1)}, u32[]{:S(2)}, u32[]{:S(2)}) %collective-permute-start.47) | collective-permute-done | bytes 32800 | tf_op jit(solution)/shard_map/ppermute | solution.py:15
  (191 shorter events, 39.1 us)
Async XLA Ops:
  0.6 25.8 %copy-start.6 = (bf16[1,128,1152]{2,1,0:T(8,128)(2,1)S(1)}, bf16[1,128,1152]{2,1,0:T(8,128)(2,1)}, u32[]{:S(2)}) copy-start(bf16[1,128,1152]{2,1,0:T(8,128)(2,1)} %param.4) | copy-start | bytes 884740
  0.6 19.2 %collective-permute-start = (bf16[1,128,1152]{2,1,0:T(8,128)(2,1)}, bf16[1,128,1152]{2,1,0:T(8,128)(2,1)S(1)}, u32[]{:S(2)}, u32[]{:S(2)}) collective-permute-start(bf16[1,128,1152]{2,1,0:T(8,128)(2,1)} %param.4), channel_id=1, source_target_pairs={{0,4},{1,5},{2,6},{3,7},{4,8},{5,9},{6,10},{7,11},{8,12},{9,13},{1... | collective-permute-start | bytes 884744 | tf_op jit(solution)/shard_map/ppermute | solution.py:15
  4.2 18.9 %collective-permute-start.1 = (bf16[1,128,1152]{2,1,0:T(8,128)(2,1)}, bf16[1,128,1152]{2,1,0:T(8,128)(2,1)S(1)}, u32[]{:S(2)}, u32[]{:S(2)}) collective-permute-start(bf16[1,128,1152]{2,1,0:T(8,128)(2,1)} %param.4), channel_id=1, source_target_pairs={{0,3},{1,4},{2,5},{3,6},{4,7},{5,8},{6,9},{7,10},{8,11},{9,12},{10... | collective-permute-start | bytes 884744 | tf_op jit(solution)/shard_map/ppermute | solution.py:15
  6.8 19.6 %collective-permute-start.2 = (bf16[1,128,1152]{2,1,0:T(8,128)(2,1)}, bf16[1,128,1152]{2,1,0:T(8,128)(2,1)S(1)}, u32[]{:S(2)}, u32[]{:S(2)}) collective-permute-start(bf16[1,128,1152]{2,1,0:T(8,128)(2,1)} %param.4), channel_id=1, source_target_pairs={{0,2},{1,3},{2,4},{3,5},{4,6},{5,7},{6,8},{7,9},{8,10},{9,11},{10,... | collective-permute-start | bytes 884744 | tf_op jit(solution)/shard_map/ppermute | solution.py:15
  10.2 20.3 %collective-permute-start.3 = (bf16[1,128,1152]{2,1,0:T(8,128)(2,1)}, bf16[1,128,1152]{2,1,0:T(8,128)(2,1)S(1)}, u32[]{:S(2)}, u32[]{:S(2)}) collective-permute-start(bf16[1,128,1152]{2,1,0:T(8,128)(2,1)} %param.4), channel_id=1, source_target_pairs={{0,1},{1,2},{2,3},{3,4},{4,5},{5,6},{6,7},{7,8},{8,9},{9,10},{10,1... | collective-permute-start | bytes 884744 | tf_op jit(solution)/shard_map/ppermute | solution.py:15
  12.8 19.1 %collective-permute-start.4 = (bf16[1,128,1152]{2,1,0:T(8,128)(2,1)}, bf16[1,128,1152]{2,1,0:T(8,128)(2,1)S(1)}, u32[]{:S(2)}, u32[]{:S(2)}) collective-permute-start(bf16[1,128,1152]{2,1,0:T(8,128)(2,1)} %param.4), channel_id=1, source_target_pairs={{1,0},{2,1},{3,2},{4,3},{5,4},{6,5},{7,6},{8,7},{9,8},{10,9},{11,1... | collective-permute-start | bytes 884744 | tf_op jit(solution)/shard_map/ppermute | solution.py:15
  17.8 33.2 %copy-start.7 = (bf16[1,128,1152]{1,2,0:T(8,128)(2,1)}, bf16[1,128,1152]{1,2,0:T(8,128)(2,1)S(1)}, u32[]{:S(2)}) copy-start(bf16[1,128,1152]{1,2,0:T(8,128)(2,1)S(1)} %copy.66) | copy-start | bytes 884740
  19.9 21.1 %collective-permute-start.5 = (bf16[1,128,1152]{2,1,0:T(8,128)(2,1)}, bf16[1,128,1152]{2,1,0:T(8,128)(2,1)S(1)}, u32[]{:S(2)}, u32[]{:S(2)}) collective-permute-start(bf16[1,128,1152]{2,1,0:T(8,128)(2,1)} %param.4), channel_id=1, source_target_pairs={{2,0},{3,1},{4,2},{5,3},{6,4},{7,5},{8,6},{9,7},{10,8},{11,9},{12,... | collective-permute-start | bytes 884744 | tf_op jit(solution)/shard_map/ppermute | solution.py:15
  23.1 18.6 %collective-permute-start.6 = (bf16[1,128,1152]{2,1,0:T(8,128)(2,1)}, bf16[1,128,1152]{2,1,0:T(8,128)(2,1)S(1)}, u32[]{:S(2)}, u32[]{:S(2)}) collective-permute-start(bf16[1,128,1152]{2,1,0:T(8,128)(2,1)} %param.4), channel_id=1, source_target_pairs={{3,0},{4,1},{5,2},{6,3},{7,4},{8,5},{9,6},{10,7},{11,8},{12,9},{13... | collective-permute-start | bytes 884744 | tf_op jit(solution)/shard_map/ppermute | solution.py:15
  26.5 17.9 %collective-permute-start.7 = (bf16[1,128,1152]{2,1,0:T(8,128)(2,1)S(1)}, bf16[1,128,1152]{2,1,0:T(8,128)(2,1)S(1)}, u32[]{:S(2)}, u32[]{:S(2)}) collective-permute-start(bf16[1,128,1152]{2,1,0:T(8,128)(2,1)S(1)} %copy-done.6), channel_id=1, source_target_pairs={{4,0},{5,1},{6,2},{7,3},{8,4},{9,5},{10,6},{11,7},{12,8},{13,9},{1... | collective-permute-start | bytes 884744 | tf_op jit(solution)/shard_map/ppermute | solution.py:15
  51.6 40.5 %copy-start.3 = (bf16[1,128,9,128]{1,3,2,0:T(8,128)(2,1)}, bf16[1,128,9,128]{1,3,2,0:T(8,128)(2,1)S(1)}, u32[]{:S(2)}) copy-start(bf16[1,128,9,128]{1,3,2,0:T(8,128)(2,1)S(1)} %multiply_convert_fusion.5) | copy-start | bytes 884740
  51.6 21.4 %collective-permute-start.13 = (bf16[1,128,1152]{1,2,0:T(8,128)(2,1)S(1)}, bf16[1,128,1152]{1,2,0:T(8,128)(2,1)}, u32[]{:S(2)}, u32[]{:S(2)}) collective-permute-start(bf16[1,128,1152]{1,2,0:T(8,128)(2,1)S(1)} %bitcast.725), channel_id=1, source_target_pairs={{2,0},{3,1},{4,2},{5,3},{6,4},{7,5},{8,6},{9,7},{10,8},{11,9},{12,... | collective-permute-start | bytes 884744 | tf_op jit(solution)/shard_map/ppermute | solution.py:15
  53.5 22.5 %collective-permute-start.10 = (bf16[1,128,1152]{1,2,0:T(8,128)(2,1)S(1)}, bf16[1,128,1152]{1,2,0:T(8,128)(2,1)}, u32[]{:S(2)}, u32[]{:S(2)}) collective-permute-start(bf16[1,128,1152]{1,2,0:T(8,128)(2,1)S(1)} %bitcast.726), channel_id=1, source_target_pairs={{0,2},{1,3},{2,4},{3,5},{4,6},{5,7},{6,8},{7,9},{8,10},{9,11},{10,... | collective-permute-start | bytes 884744 | tf_op jit(solution)/shard_map/ppermute | solution.py:15
  57.4 21.6 %collective-permute-start.14 = (bf16[1,128,1152]{1,2,0:T(8,128)(2,1)S(1)}, bf16[1,128,1152]{1,2,0:T(8,128)(2,1)}, u32[]{:S(2)}, u32[]{:S(2)}) collective-permute-start(bf16[1,128,1152]{1,2,0:T(8,128)(2,1)S(1)} %bitcast.727), channel_id=1, source_target_pairs={{3,0},{4,1},{5,2},{6,3},{7,4},{8,5},{9,6},{10,7},{11,8},{12,9},{13... | collective-permute-start | bytes 884744 | tf_op jit(solution)/shard_map/ppermute | solution.py:15
  60.5 30.1 %collective-permute-start.12 = (bf16[1,128,1152]{1,2,0:T(8,128)(2,1)S(1)}, bf16[1,128,1152]{1,2,0:T(8,128)(2,1)S(1)}, u32[]{:S(2)}, u32[]{:S(2)}) collective-permute-start(bf16[1,128,1152]{1,2,0:T(8,128)(2,1)S(1)} %bitcast.728), channel_id=1, source_target_pairs={{1,0},{2,1},{3,2},{4,3},{5,4},{6,5},{7,6},{8,7},{9,8},{10,9},{11,1... | collective-permute-start | bytes 884744 | tf_op jit(solution)/shard_map/ppermute | solution.py:15
  63.2 27.6 %collective-permute-start.11 = (bf16[1,128,1152]{1,2,0:T(8,128)(2,1)S(1)}, bf16[1,128,1152]{1,2,0:T(8,128)(2,1)S(1)}, u32[]{:S(2)}, u32[]{:S(2)}) collective-permute-start(bf16[1,128,1152]{1,2,0:T(8,128)(2,1)S(1)} %bitcast.729), channel_id=1, source_target_pairs={{0,1},{1,2},{2,3},{3,4},{4,5},{5,6},{6,7},{7,8},{8,9},{9,10},{10,1... | collective-permute-start | bytes 884744 | tf_op jit(solution)/shard_map/ppermute | solution.py:15
  72.9 16.1 %collective-permute-start.9 = (bf16[1,128,1152]{1,2,0:T(8,128)(2,1)S(1)}, bf16[1,128,1152]{1,2,0:T(8,128)(2,1)S(1)}, u32[]{:S(2)}, u32[]{:S(2)}) collective-permute-start(bf16[1,128,1152]{1,2,0:T(8,128)(2,1)S(1)} %bitcast.730), channel_id=1, source_target_pairs={{0,3},{1,4},{2,5},{3,6},{4,7},{5,8},{6,9},{7,10},{8,11},{9,12},{10... | collective-permute-start | bytes 884744 | tf_op jit(solution)/shard_map/ppermute | solution.py:15
  76.0 14.5 %collective-permute-start.15 = (bf16[1,128,1152]{1,2,0:T(8,128)(2,1)S(1)}, bf16[1,128,1152]{1,2,0:T(8,128)(2,1)S(1)}, u32[]{:S(2)}, u32[]{:S(2)}) collective-permute-start(bf16[1,128,1152]{1,2,0:T(8,128)(2,1)S(1)} %bitcast.731), channel_id=1, source_target_pairs={{4,0},{5,1},{6,2},{7,3},{8,4},{9,5},{10,6},{11,7},{12,8},{13,9},{1... | collective-permute-start | bytes 884744 | tf_op jit(solution)/shard_map/ppermute | solution.py:15
  79.1 12.8 %collective-permute-start.8 = (bf16[1,128,1152]{1,2,0:T(8,128)(2,1)S(1)}, bf16[1,128,1152]{1,2,0:T(8,128)(2,1)S(1)}, u32[]{:S(2)}, u32[]{:S(2)}) collective-permute-start(bf16[1,128,1152]{1,2,0:T(8,128)(2,1)S(1)} %bitcast.732), channel_id=1, source_target_pairs={{0,4},{1,5},{2,6},{3,7},{4,8},{5,9},{6,10},{7,11},{8,12},{9,13},{1... | collective-permute-start | bytes 884744 | tf_op jit(solution)/shard_map/ppermute | solution.py:15
  93.0 17.2 %collective-permute-start.16 = (bf16[1,128,128]{1,2,0:T(8,128)(2,1)S(1)}, bf16[1,128,128]{1,2,0:T(8,128)(2,1)S(1)}, u32[]{:S(2)}, u32[]{:S(2)}) collective-permute-start(bf16[1,128,128]{1,2,0:T(8,128)(2,1)S(1)} %get-tuple-element.29), channel_id=1, source_target_pairs={{0,4},{1,5},{2,6},{3,7},{4,8},{5,9},{6,10},{7,11},{8,12},{9,13},{1... | collective-permute-start | bytes 98312 | tf_op jit(solution)/shard_map/ppermute | solution.py:15
  96.2 18.6 %collective-permute-start.17 = (bf16[1,128,128]{1,2,0:T(8,128)(2,1)}, bf16[1,128,128]{1,2,0:T(8,128)(2,1)S(1)}, u32[]{:S(2)}, u32[]{:S(2)}) collective-permute-start(bf16[1,128,128]{1,2,0:T(8,128)(2,1)} %get-tuple-element.28), channel_id=1, source_target_pairs={{0,3},{1,4},{2,5},{3,6},{4,7},{5,8},{6,9},{7,10},{8,11},{9,12},{10... | collective-permute-start | bytes 98312 | tf_op jit(solution)/shard_map/ppermute | solution.py:15
  101.1 15.6 %collective-permute-start.18 = (bf16[1,128,128]{1,2,0:T(8,128)(2,1)}, bf16[1,128,128]{1,2,0:T(8,128)(2,1)S(1)}, u32[]{:S(2)}, u32[]{:S(2)}) collective-permute-start(bf16[1,128,128]{1,2,0:T(8,128)(2,1)} %get-tuple-element.27), channel_id=1, source_target_pairs={{0,2},{1,3},{2,4},{3,5},{4,6},{5,7},{6,8},{7,9},{8,10},{9,11},{10,... | collective-permute-start | bytes 98312 | tf_op jit(solution)/shard_map/ppermute | solution.py:15
  103.7 15.9 %collective-permute-start.19 = (bf16[1,128,128]{1,2,0:T(8,128)(2,1)}, bf16[1,128,128]{1,2,0:T(8,128)(2,1)S(1)}, u32[]{:S(2)}, u32[]{:S(2)}) collective-permute-start(bf16[1,128,128]{1,2,0:T(8,128)(2,1)} %get-tuple-element.26), channel_id=1, source_target_pairs={{0,1},{1,2},{2,3},{3,4},{4,5},{5,6},{6,7},{7,8},{8,9},{9,10},{10,1... | collective-permute-start | bytes 98312 | tf_op jit(solution)/shard_map/ppermute | solution.py:15
  105.6 14.0 %collective-permute-start.20 = (bf16[1,128,128]{1,2,0:T(8,128)(2,1)}, bf16[1,128,128]{1,2,0:T(8,128)(2,1)S(1)}, u32[]{:S(2)}, u32[]{:S(2)}) collective-permute-start(bf16[1,128,128]{1,2,0:T(8,128)(2,1)} %get-tuple-element.25), channel_id=1, source_target_pairs={{1,0},{2,1},{3,2},{4,3},{5,4},{6,5},{7,6},{8,7},{9,8},{10,9},{11,1... | collective-permute-start | bytes 98312 | tf_op jit(solution)/shard_map/ppermute | solution.py:15
  110.8 8.9 %collective-permute-start.21 = (bf16[1,128,128]{1,2,0:T(8,128)(2,1)}, bf16[1,128,128]{1,2,0:T(8,128)(2,1)S(1)}, u32[]{:S(2)}, u32[]{:S(2)}) collective-permute-start(bf16[1,128,128]{1,2,0:T(8,128)(2,1)} %get-tuple-element.24), channel_id=1, source_target_pairs={{2,0},{3,1},{4,2},{5,3},{6,4},{7,5},{8,6},{9,7},{10,8},{11,9},{12,... | collective-permute-start | bytes 98312 | tf_op jit(solution)/shard_map/ppermute | solution.py:15
  114.8 5.4 %collective-permute-start.22 = (bf16[1,128,128]{1,2,0:T(8,128)(2,1)}, bf16[1,128,128]{1,2,0:T(8,128)(2,1)S(1)}, u32[]{:S(2)}, u32[]{:S(2)}) collective-permute-start(bf16[1,128,128]{1,2,0:T(8,128)(2,1)} %get-tuple-element.23), channel_id=1, source_target_pairs={{3,0},{4,1},{5,2},{6,3},{7,4},{8,5},{9,6},{10,7},{11,8},{12,9},{13... | collective-permute-start | bytes 98312 | tf_op jit(solution)/shard_map/ppermute | solution.py:15
  116.8 7.2 %collective-permute-start.23 = (bf16[1,128,128]{1,2,0:T(8,128)(2,1)}, bf16[1,128,128]{1,2,0:T(8,128)(2,1)S(1)}, u32[]{:S(2)}, u32[]{:S(2)}) collective-permute-start(bf16[1,128,128]{1,2,0:T(8,128)(2,1)} %get-tuple-element.22), channel_id=1, source_target_pairs={{4,0},{5,1},{6,2},{7,3},{8,4},{9,5},{10,6},{11,7},{12,8},{13,9},{1... | collective-permute-start | bytes 98312 | tf_op jit(solution)/shard_map/ppermute | solution.py:15
  126.9 33.9 %copy-start.4 = (bf16[1,128,9,128]{1,3,2,0:T(8,128)(2,1)S(1)}, bf16[1,128,9,128]{1,3,2,0:T(8,128)(2,1)}, u32[]{:S(2)}) copy-start(bf16[1,128,9,128]{1,3,2,0:T(8,128)(2,1)} %copy-done.3) | copy-start | bytes 884740
  126.9 15.5 %collective-permute-start.26 = (bf16[1,128,1152]{1,2,0:T(8,128)(2,1)S(1)}, bf16[1,128,1152]{1,2,0:T(8,128)(2,1)S(1)}, u32[]{:S(2)}, u32[]{:S(2)}) collective-permute-start(bf16[1,128,1152]{1,2,0:T(8,128)(2,1)S(1)} %multiply_convert_fusion.3), channel_id=1, source_target_pairs={{0,2},{1,3},{2,4},{3,5},{4,6},{5,7},{6,8},{7,9},{8,10},{9,11},{10,... | collective-permute-start | bytes 884744 | tf_op jit(solution)/shard_map/ppermute | solution.py:15
  129.4 21.3 %collective-permute-start.29 = (bf16[1,128,1152]{1,2,0:T(8,128)(2,1)S(1)}, bf16[1,128,1152]{1,2,0:T(8,128)(2,1)S(1)}, u32[]{:S(2)}, u32[]{:S(2)}) collective-permute-start(bf16[1,128,1152]{1,2,0:T(8,128)(2,1)S(1)} %multiply_convert_fusion.3), channel_id=1, source_target_pairs={{2,0},{3,1},{4,2},{5,3},{6,4},{7,5},{8,6},{9,7},{10,8},{11,9},{12,... | collective-permute-start | bytes 884744 | tf_op jit(solution)/shard_map/ppermute | solution.py:15
  133.8 24.0 %collective-permute-start.25 = (bf16[1,128,1152]{1,2,0:T(8,128)(2,1)S(1)}, bf16[1,128,1152]{1,2,0:T(8,128)(2,1)S(1)}, u32[]{:S(2)}, u32[]{:S(2)}) collective-permute-start(bf16[1,128,1152]{1,2,0:T(8,128)(2,1)S(1)} %multiply_convert_fusion.3), channel_id=1, source_target_pairs={{0,3},{1,4},{2,5},{3,6},{4,7},{5,8},{6,9},{7,10},{8,11},{9,12},{10... | collective-permute-start | bytes 884744 | tf_op jit(solution)/shard_map/ppermute | solution.py:15
  135.8 25.2 %collective-permute-start.24 = (bf16[1,128,1152]{1,2,0:T(8,128)(2,1)S(1)}, bf16[1,128,1152]{1,2,0:T(8,128)(2,1)S(1)}, u32[]{:S(2)}, u32[]{:S(2)}) collective-permute-start(bf16[1,128,1152]{1,2,0:T(8,128)(2,1)S(1)} %multiply_convert_fusion.3), channel_id=1, source_target_pairs={{0,4},{1,5},{2,6},{3,7},{4,8},{5,9},{6,10},{7,11},{8,12},{9,13},{1... | collective-permute-start | bytes 884744 | tf_op jit(solution)/shard_map/ppermute | solution.py:15
  138.7 22.5 %collective-permute-start.27 = (bf16[1,128,1152]{1,2,0:T(8,128)(2,1)S(1)}, bf16[1,128,1152]{1,2,0:T(8,128)(2,1)S(1)}, u32[]{:S(2)}, u32[]{:S(2)}) collective-permute-start(bf16[1,128,1152]{1,2,0:T(8,128)(2,1)S(1)} %multiply_convert_fusion.3), channel_id=1, source_target_pairs={{0,1},{1,2},{2,3},{3,4},{4,5},{5,6},{6,7},{7,8},{8,9},{9,10},{10,1... | collective-permute-start | bytes 884744 | tf_op jit(solution)/shard_map/ppermute | solution.py:15
  142.4 18.8 %copy-start.17 = (bf16[1,128,1152]{1,2,0:T(8,128)(2,1)}, bf16[1,128,1152]{1,2,0:T(8,128)(2,1)S(1)}, u32[]{:S(2)}) copy-start(bf16[1,128,1152]{1,2,0:T(8,128)(2,1)S(1)} %collective-permute-done.26) | copy-start | bytes 884740
  142.4 18.3 %collective-permute-start.30 = (bf16[1,128,1152]{1,2,0:T(8,128)(2,1)S(1)}, bf16[1,128,1152]{1,2,0:T(8,128)(2,1)S(1)}, u32[]{:S(2)}, u32[]{:S(2)}) collective-permute-start(bf16[1,128,1152]{1,2,0:T(8,128)(2,1)S(1)} %multiply_convert_fusion.3), channel_id=1, source_target_pairs={{3,0},{4,1},{5,2},{6,3},{7,4},{8,5},{9,6},{10,7},{11,8},{12,9},{13... | collective-permute-start | bytes 884744 | tf_op jit(solution)/shard_map/ppermute | solution.py:15
  145.5 22.8 %copy-start.1 = (bf16[1,128,9,128]{3,1,2,0:T(8,128)(2,1)S(1)}, bf16[1,128,9,128]{3,1,2,0:T(8,128)(2,1)}, u32[]{:S(2)}) copy-start(bf16[1,128,9,128]{3,1,2,0:T(8,128)(2,1)} %copy-done) | copy-start | bytes 884740
  150.7 10.5 %copy-start.15 = (bf16[1,128,1152]{1,2,0:T(8,128)(2,1)}, bf16[1,128,1152]{1,2,0:T(8,128)(2,1)S(1)}, u32[]{:S(2)}) copy-start(bf16[1,128,1152]{1,2,0:T(8,128)(2,1)S(1)} %collective-permute-done.29) | copy-start | bytes 884740
  150.7 11.1 %collective-permute-start.28 = (bf16[1,128,1152]{1,2,0:T(8,128)(2,1)S(1)}, bf16[1,128,1152]{1,2,0:T(8,128)(2,1)S(1)}, u32[]{:S(2)}, u32[]{:S(2)}) collective-permute-start(bf16[1,128,1152]{1,2,0:T(8,128)(2,1)S(1)} %multiply_convert_fusion.3), channel_id=1, source_target_pairs={{1,0},{2,1},{3,2},{4,3},{5,4},{6,5},{7,6},{8,7},{9,8},{10,9},{11,1... | collective-permute-start | bytes 884744 | tf_op jit(solution)/shard_map/ppermute | solution.py:15
  157.9 3.9 %copy-start.19 = (bf16[1,128,1152]{1,2,0:T(8,128)(2,1)}, bf16[1,128,1152]{1,2,0:T(8,128)(2,1)S(1)}, u32[]{:S(2)}) copy-start(bf16[1,128,1152]{1,2,0:T(8,128)(2,1)S(1)} %collective-permute-done.25) | copy-start | bytes 884740
  157.9 9.5 %collective-permute-start.31 = (bf16[1,128,1152]{1,2,0:T(8,128)(2,1)S(1)}, bf16[1,128,1152]{1,2,0:T(8,128)(2,1)S(1)}, u32[]{:S(2)}, u32[]{:S(2)}) collective-permute-start(bf16[1,128,1152]{1,2,0:T(8,128)(2,1)S(1)} %multiply_convert_fusion.3), channel_id=1, source_target_pairs={{4,0},{5,1},{6,2},{7,3},{8,4},{9,5},{10,6},{11,7},{12,8},{13,9},{1... | collective-permute-start | bytes 884744 | tf_op jit(solution)/shard_map/ppermute | solution.py:15
  160.8 6.6 %copy-start.21 = (bf16[1,128,1152]{1,2,0:T(8,128)(2,1)}, bf16[1,128,1152]{1,2,0:T(8,128)(2,1)S(1)}, u32[]{:S(2)}) copy-start(bf16[1,128,1152]{1,2,0:T(8,128)(2,1)S(1)} %collective-permute-done.30) | copy-start | bytes 884740
  161.0 6.4 %copy-start.23 = (bf16[1,128,1152]{1,2,0:T(8,128)(2,1)}, bf16[1,128,1152]{1,2,0:T(8,128)(2,1)S(1)}, u32[]{:S(2)}) copy-start(bf16[1,128,1152]{1,2,0:T(8,128)(2,1)S(1)} %collective-permute-done.24) | copy-start | bytes 884740
  161.2 6.2 %copy-start.11 = (bf16[1,128,1152]{1,2,0:T(8,128)(2,1)}, bf16[1,128,1152]{1,2,0:T(8,128)(2,1)S(1)}, u32[]{:S(2)}) copy-start(bf16[1,128,1152]{1,2,0:T(8,128)(2,1)S(1)} %collective-permute-done.27) | copy-start | bytes 884740
  161.8 5.6 %copy-start.13 = (bf16[1,128,1152]{1,2,0:T(8,128)(2,1)}, bf16[1,128,1152]{1,2,0:T(8,128)(2,1)S(1)}, u32[]{:S(2)}) copy-start(bf16[1,128,1152]{1,2,0:T(8,128)(2,1)S(1)} %collective-permute-done.28) | copy-start | bytes 884740
  170.1 18.1 %collective-permute-start.32 = (bf16[1,128,128]{1,2,0:T(8,128)(2,1)}, bf16[1,128,128]{1,2,0:T(8,128)(2,1)}, u32[]{:S(2)}, u32[]{:S(2)}) collective-permute-start(bf16[1,128,128]{1,2,0:T(8,128)(2,1)} %get-tuple-element.21), channel_id=1, source_target_pairs={{0,4},{1,5},{2,6},{3,7},{4,8},{5,9},{6,10},{7,11},{8,12},{9,13},{1... | collective-permute-start | bytes 98312 | tf_op jit(solution)/shard_map/ppermute | solution.py:15
  176.9 15.0 %collective-permute-start.33 = (bf16[1,128,128]{1,2,0:T(8,128)(2,1)}, bf16[1,128,128]{1,2,0:T(8,128)(2,1)S(1)}, u32[]{:S(2)}, u32[]{:S(2)}) collective-permute-start(bf16[1,128,128]{1,2,0:T(8,128)(2,1)} %get-tuple-element.20), channel_id=1, source_target_pairs={{0,3},{1,4},{2,5},{3,6},{4,7},{5,8},{6,9},{7,10},{8,11},{9,12},{10... | collective-permute-start | bytes 98312 | tf_op jit(solution)/shard_map/ppermute | solution.py:15
  178.8 16.3 %collective-permute-start.34 = (bf16[1,128,128]{1,2,0:T(8,128)(2,1)}, bf16[1,128,128]{1,2,0:T(8,128)(2,1)S(1)}, u32[]{:S(2)}, u32[]{:S(2)}) collective-permute-start(bf16[1,128,128]{1,2,0:T(8,128)(2,1)} %get-tuple-element.19), channel_id=1, source_target_pairs={{0,2},{1,3},{2,4},{3,5},{4,6},{5,7},{6,8},{7,9},{8,10},{9,11},{10,... | collective-permute-start | bytes 98312 | tf_op jit(solution)/shard_map/ppermute | solution.py:15
  181.2 17.6 %collective-permute-start.35 = (bf16[1,128,128]{1,2,0:T(8,128)(2,1)}, bf16[1,128,128]{1,2,0:T(8,128)(2,1)S(1)}, u32[]{:S(2)}, u32[]{:S(2)}) collective-permute-start(bf16[1,128,128]{1,2,0:T(8,128)(2,1)} %get-tuple-element.18), channel_id=1, source_target_pairs={{0,1},{1,2},{2,3},{3,4},{4,5},{5,6},{6,7},{7,8},{8,9},{9,10},{10,1... | collective-permute-start | bytes 98312 | tf_op jit(solution)/shard_map/ppermute | solution.py:15
  184.0 15.6 %collective-permute-start.36 = (bf16[1,128,128]{1,2,0:T(8,128)(2,1)}, bf16[1,128,128]{1,2,0:T(8,128)(2,1)S(1)}, u32[]{:S(2)}, u32[]{:S(2)}) collective-permute-start(bf16[1,128,128]{1,2,0:T(8,128)(2,1)} %get-tuple-element.17), channel_id=1, source_target_pairs={{1,0},{2,1},{3,2},{4,3},{5,4},{6,5},{7,6},{8,7},{9,8},{10,9},{11,1... | collective-permute-start | bytes 98312 | tf_op jit(solution)/shard_map/ppermute | solution.py:15
  188.2 11.4 %collective-permute-start.37 = (bf16[1,128,128]{1,2,0:T(8,128)(2,1)}, bf16[1,128,128]{1,2,0:T(8,128)(2,1)S(1)}, u32[]{:S(2)}, u32[]{:S(2)}) collective-permute-start(bf16[1,128,128]{1,2,0:T(8,128)(2,1)} %get-tuple-element.16), channel_id=1, source_target_pairs={{2,0},{3,1},{4,2},{5,3},{6,4},{7,5},{8,6},{9,7},{10,8},{11,9},{12,... | collective-permute-start | bytes 98312 | tf_op jit(solution)/shard_map/ppermute | solution.py:15
  191.9 7.7 %collective-permute-start.38 = (bf16[1,128,128]{1,2,0:T(8,128)(2,1)}, bf16[1,128,128]{1,2,0:T(8,128)(2,1)S(1)}, u32[]{:S(2)}, u32[]{:S(2)}) collective-permute-start(bf16[1,128,128]{1,2,0:T(8,128)(2,1)} %get-tuple-element.15), channel_id=1, source_target_pairs={{3,0},{4,1},{5,2},{6,3},{7,4},{8,5},{9,6},{10,7},{11,8},{12,9},{13... | collective-permute-start | bytes 98312 | tf_op jit(solution)/shard_map/ppermute | solution.py:15
  195.1 6.9 %collective-permute-start.39 = (bf16[1,128,128]{1,2,0:T(8,128)(2,1)}, bf16[1,128,128]{1,2,0:T(8,128)(2,1)S(1)}, u32[]{:S(2)}, u32[]{:S(2)}) collective-permute-start(bf16[1,128,128]{1,2,0:T(8,128)(2,1)} %get-tuple-element.14), channel_id=1, source_target_pairs={{4,0},{5,1},{6,2},{7,3},{8,4},{9,5},{10,6},{11,7},{12,8},{13,9},{1... | collective-permute-start | bytes 98312 | tf_op jit(solution)/shard_map/ppermute | solution.py:15
  203.9 1.7 copy-start.10
  206.2 1.8 copy-start.2
  207.9 16.0 %copy-start.9 = (f32[1,128,9,128]{3,1,2,0:T(8,128)S(1)}, f32[1,128,9,128]{3,1,2,0:T(8,128)}, u32[]{:S(2)}) copy-start(f32[1,128,9,128]{3,1,2,0:T(8,128)} %get-tuple-element.4) | copy-start | bytes 1769476
  208.3 15.9 %collective-permute-start.40 = (bf16[1,128,128]{1,2,0:T(8,128)(2,1)S(1)}, bf16[1,128,128]{1,2,0:T(8,128)(2,1)S(1)}, u32[]{:S(2)}, u32[]{:S(2)}) collective-permute-start(bf16[1,128,128]{1,2,0:T(8,128)(2,1)S(1)} %get-tuple-element.13), channel_id=1, source_target_pairs={{0,4},{1,5},{2,6},{3,7},{4,8},{5,9},{6,10},{7,11},{8,12},{9,13},{1... | collective-permute-start | bytes 98312 | tf_op jit(solution)/shard_map/ppermute | solution.py:15
  211.4 26.1 %copy-start.8 = (bf16[1,128,1152]{1,2,0:T(8,128)(2,1)S(1)}, bf16[1,128,1152]{1,2,0:T(8,128)(2,1)}, u32[]{:S(2)}) copy-start(bf16[1,128,1152]{1,2,0:T(8,128)(2,1)} %copy-done.7) | copy-start | bytes 884740
  211.6 14.8 %collective-permute-start.41 = (bf16[1,128,128]{1,2,0:T(8,128)(2,1)S(1)}, bf16[1,128,128]{1,2,0:T(8,128)(2,1)S(1)}, u32[]{:S(2)}, u32[]{:S(2)}) collective-permute-start(bf16[1,128,128]{1,2,0:T(8,128)(2,1)S(1)} %get-tuple-element.12), channel_id=1, source_target_pairs={{0,3},{1,4},{2,5},{3,6},{4,7},{5,8},{6,9},{7,10},{8,11},{9,12},{10... | collective-permute-start | bytes 98312 | tf_op jit(solution)/shard_map/ppermute | solution.py:15
  213.8 16.6 %collective-permute-start.42 = (bf16[1,128,128]{1,2,0:T(8,128)(2,1)S(1)}, bf16[1,128,128]{1,2,0:T(8,128)(2,1)S(1)}, u32[]{:S(2)}, u32[]{:S(2)}) collective-permute-start(bf16[1,128,128]{1,2,0:T(8,128)(2,1)S(1)} %get-tuple-element.11), channel_id=1, source_target_pairs={{0,2},{1,3},{2,4},{3,5},{4,6},{5,7},{6,8},{7,9},{8,10},{9,11},{10,... | collective-permute-start | bytes 98312 | tf_op jit(solution)/shard_map/ppermute | solution.py:15
  217.5 16.6 %collective-permute-start.43 = (bf16[1,128,128]{1,2,0:T(8,128)(2,1)S(1)}, bf16[1,128,128]{1,2,0:T(8,128)(2,1)S(1)}, u32[]{:S(2)}, u32[]{:S(2)}) collective-permute-start(bf16[1,128,128]{1,2,0:T(8,128)(2,1)S(1)} %get-tuple-element.10), channel_id=1, source_target_pairs={{0,1},{1,2},{2,3},{3,4},{4,5},{5,6},{6,7},{7,8},{8,9},{9,10},{10,1... | collective-permute-start | bytes 98312 | tf_op jit(solution)/shard_map/ppermute | solution.py:15
  219.4 14.7 %collective-permute-start.44 = (bf16[1,128,128]{1,2,0:T(8,128)(2,1)S(1)}, bf16[1,128,128]{1,2,0:T(8,128)(2,1)S(1)}, u32[]{:S(2)}, u32[]{:S(2)}) collective-permute-start(bf16[1,128,128]{1,2,0:T(8,128)(2,1)S(1)} %get-tuple-element.9), channel_id=1, source_target_pairs={{1,0},{2,1},{3,2},{4,3},{5,4},{6,5},{7,6},{8,7},{9,8},{10,9},{11,1... | collective-permute-start | bytes 98312 | tf_op jit(solution)/shard_map/ppermute | solution.py:15
  224.2 9.9 %collective-permute-start.45 = (bf16[1,128,128]{1,2,0:T(8,128)(2,1)S(1)}, bf16[1,128,128]{1,2,0:T(8,128)(2,1)S(1)}, u32[]{:S(2)}, u32[]{:S(2)}) collective-permute-start(bf16[1,128,128]{1,2,0:T(8,128)(2,1)S(1)} %get-tuple-element.8), channel_id=1, source_target_pairs={{2,0},{3,1},{4,2},{5,3},{6,4},{7,5},{8,6},{9,7},{10,8},{11,9},{12,... | collective-permute-start | bytes 98312 | tf_op jit(solution)/shard_map/ppermute | solution.py:15
  226.4 7.8 %collective-permute-start.46 = (bf16[1,128,128]{1,2,0:T(8,128)(2,1)S(1)}, bf16[1,128,128]{1,2,0:T(8,128)(2,1)S(1)}, u32[]{:S(2)}, u32[]{:S(2)}) collective-permute-start(bf16[1,128,128]{1,2,0:T(8,128)(2,1)S(1)} %get-tuple-element.7), channel_id=1, source_target_pairs={{3,0},{4,1},{5,2},{6,3},{7,4},{8,5},{9,6},{10,7},{11,8},{12,9},{13... | collective-permute-start | bytes 98312 | tf_op jit(solution)/shard_map/ppermute | solution.py:15
  230.4 6.7 %collective-permute-start.47 = (bf16[1,128,128]{1,2,0:T(8,128)(2,1)S(1)}, bf16[1,128,128]{1,2,0:T(8,128)(2,1)S(1)}, u32[]{:S(2)}, u32[]{:S(2)}) collective-permute-start(bf16[1,128,128]{1,2,0:T(8,128)(2,1)S(1)} %get-tuple-element.6), channel_id=1, source_target_pairs={{4,0},{5,1},{6,2},{7,3},{8,4},{9,5},{10,6},{11,7},{12,8},{13,9},{1... | collective-permute-start | bytes 98312 | tf_op jit(solution)/shard_map/ppermute | solution.py:15
  (12 other events, 12.4 us)
where the time goes:
time: 242 us; the launch traced here: 239 us
  starting transfers between devices  141 us (58%)
  waiting for transfers between devices  47.4 us (20%)
  local copies, waits for them, and re-layouts  28.5 us (12%)
  matrix products  15.6 us (6%)
  other arithmetic  3.93 us (2%)
    ppermute x48, starting transfers between devices, shifted(): lax.ppermute(value, axis, [(source, source + steps) for source in range(i...  141 us
    ppermute x48, waiting for transfers between devices, shifted(): lax.ppermute(value, axis, [(source, source + steps) for source in range(i...  47.4 us
    unnamed x93, local copies, waits for them, and re-layouts  17.8 us
    dot_general x44, matrix products, band_product(): jnp.einsum('rik,rkqc->riqc', left_blocks[:, :, p, :], right_blocks[p:p +...  14.3 us
    concatenate x2, local copies, waits for them, and re-layouts, extend(): joined = jnp.concatenate(below + [local_rows] + above, axis=0)  5.27 us
  transfers between devices with their start and end apart: 48, of which 16 were waited for; matrix products, arithmetic and copies ran while one was open for 11% of the time, Pallas kernels for 0%

commit v1 on v0

v1 whole, which is shorter than its diff:
```python
import functools

import jax
import jax.numpy as jnp
from jax import lax
from jax.experimental import pallas as pl
from jax.experimental.pallas import tpu as pltpu
from jax.sharding import PartitionSpec as P

STEP_SCALE = 0.015625
SYMMETRIC = False


def kernel(ncol, n, b, half, sym, margin, fock, density, present, grad, upd,
           sw, xw, tw, xrow, trow, dv, fv, mv, gd, gm, cf, ch, co, qd, qm,
           lsem, wsend, wrecv, msend, mrecv):
    band = 2 * half + 1
    r = lax.axis_index("row") * ncol + lax.axis_index("col")
    k = r // 2
    core = r % 2
    chips = n // 2

    def device(t):
        return {"row": t // ncol, "col": t % ncol}

    def col(i, count=1):
        return pl.ds(pl.multiple_of(i * b, b), count * b)

    def valid_chip(e):
        return jnp.logical_and(k + e >= 0, k + e < chips)

    def valid(d):
        return jnp.logical_and(r + d >= 0, r + d < n)

    sibling = device(r + 1 - 2 * core)
    offsets = [d for d in range(-half, half + 1) if d != 0]
    reach = half // 2
    hops = [e for m in range(1, reach + 1) for e in (m, -m)]

    loads = [
        pltpu.make_async_copy(margin.at[0], mv, lsem.at[0]),
        pltpu.make_async_copy(density.at[0], dv, lsem.at[1]),
        pltpu.make_async_copy(fock.at[0], fv, lsem.at[2]),
    ]
    for c in loads:
        c.start()

    barrier = pltpu.get_barrier_semaphore()
    for d in offsets:
        @pl.when(valid(d))
        def _():
            pl.semaphore_signal(barrier, inc=1, device_id=device(r + d),
                                device_id_type=pl.DeviceIdType.MESH)

    for e in hops:
        @pl.when(jnp.logical_not(valid_chip(e)))
        def _():
            p = half + 2 * e
            for w in (sw, xw, tw):
                w[p * b:(p + 2) * b, :] = jnp.zeros((2 * b, w.shape[1]), w.dtype)
    for d in offsets:
        @pl.when(jnp.logical_not(valid(-d)))
        def _():
            for m in (gm.at[0], gm.at[1], gm.at[2]):
                m[half - d] = jnp.zeros((b, b), gm.dtype)

    expected = jnp.minimum(r, half) + jnp.minimum(n - 1 - r, half)
    pl.semaphore_wait(barrier, expected)

    pending = []

    def window_plan(symmetric):
        plan = []
        for e in hops:
            if e > 0:
                s0 = 2 * e - 1
                plan.append((e, s0, band - s0, core - 1))
            else:
                plan.append((e, 0, band + 2 * e + 1, core - 2 * e))
        return plan

    def spread(phase, own, w, symmetric):
        plan = window_plan(symmetric)
        here = pl.ds(pl.multiple_of((half + core) * b, b), b)
        copies = []
        for i, (e, s0, count, c0) in enumerate(plan):
            p = half - 2 * e + core
            spot = w.at[pl.ds(pl.multiple_of(p * b, b), b), col(c0 + 1, count)]
            src = own.at[:, s0 * b:(s0 + count) * b]
            send = pltpu.make_async_remote_copy(
                src_ref=src, dst_ref=spot, send_sem=wsend.at[phase, i],
                recv_sem=wrecv.at[phase, i], device_id=device(r + 2 * e),
                device_id_type=pl.DeviceIdType.MESH)
            relay = pltpu.make_async_remote_copy(
                src_ref=spot, dst_ref=spot, send_sem=wsend.at[phase, 6 + i],
                recv_sem=wrecv.at[phase, 6 + i], device_id=sibling,
                device_id_type=pl.DeviceIdType.MESH)

            @pl.when(valid_chip(e))
            def _():
                send.start()
            copies.append((e, send, relay))
        share = pltpu.make_async_remote_copy(
            src_ref=own, dst_ref=w.at[here, col(core + 1, band)],
            send_sem=wsend.at[phase, 12], recv_sem=wrecv.at[phase, 12],
            device_id=sibling, device_id_type=pl.DeviceIdType.MESH)
        share.start()
        w[here, col(core + 1, band)] = own[...]
        for e, send, relay in copies:
            @pl.when(valid_chip(-e))
            def _():
                send.wait_recv()
                relay.start()
        share.wait_recv()
        for e, send, relay in copies:
            @pl.when(valid_chip(-e))
            def _():
                relay.wait_recv()
            pending.append((valid_chip(e), send))
            pending.append((valid_chip(-e), relay))
        pending.append((None, share))

    def mirror(phase, own, m):
        copies = []
        for i, d in enumerate(sorted(offsets, key=lambda v: -abs(v))):
            c = pltpu.make_async_remote_copy(
                src_ref=own.at[:, (half + d) * b:(half + d + 1) * b],
                dst_ref=m.at[half - d], send_sem=msend.at[phase, i],
                recv_sem=mrecv.at[phase, i], device_id=device(r + d),
                device_id_type=pl.DeviceIdType.MESH)

            @pl.when(valid(d))
            def _():
                c.start()
            copies.append((d, c))
        m[half] = own[:, half * b:(half + 1) * b]
        for d, c in copies:
            @pl.when(valid(-d))
            def _():
                c.wait_recv()
            pending.append((valid(d), c))

    def product(left, w, out):
        for c in range(band):
            lo, hi = max(0, c - half), min(band, c + half + 1)
            rhs = w[pl.ds(pl.multiple_of((core + lo) * b, b), (hi - lo) * b), col(core + 1 + c)]
            acc = jnp.dot(left[:, lo * b:hi * b], rhs, preferred_element_type=jnp.float32)
            keep = present[0, c].astype(jnp.float32)
            out[:, c * b:(c + 1) * b] = (acc * keep).astype(out.dtype)

    loads[0].wait()
    spread(0, mv, sw, sym)
    loads[1].wait()
    product(dv, sw, xrow)
    spread(1, xrow, xw, False)
    loads[2].wait()
    product(fv, xw, gd)
    mirror(0, gd, gm.at[0])
    for c in range(band):
        cols = slice(c * b, (c + 1) * b)
        g = gd[:, cols].astype(jnp.float32) - gm[0, c].T.astype(jnp.float32)
        grad[0, :, cols] = g
        trow[:, cols] = (-STEP_SCALE * g).astype(trow.dtype)
    spread(2, trow, tw, sym)
    product(xrow, tw, cf)
    mirror(1, cf, gm.at[1])
    for c in range(band):
        cols = slice(c * b, (c + 1) * b)
        v = cf[:, cols].astype(jnp.float32) + gm[1, c].T.astype(jnp.float32)
        upd[0, :, cols] = dv[:, cols].astype(jnp.float32) + v
        ch[:, cols] = v.astype(ch.dtype)
    product(ch, sw, co)
    product(co, tw, qd)
    mirror(2, qd, gm.at[2])
    for c in range(band):
        cols = slice(c * b, (c + 1) * b)
        q = qd[:, cols].astype(jnp.float32) + gm[2, c].T.astype(jnp.float32)
        upd[0, :, cols] += 0.5 * q
    for cond, c in pending:
        if cond is None:
            c.wait_send()
        else:
            @pl.when(cond)
            def _():
                c.wait_send()


def local(ncol, n, margin, fock_matrix, density, present):
    rows, b, width = margin.shape
    band = present.shape[1]
    half = (band - 1) // 2
    bf = jnp.bfloat16
    row = pltpu.VMEM((b, width), bf)
    wide = pltpu.VMEM(((band + 1) * b, (band + 3) * b), bf)
    out = jax.ShapeDtypeStruct((rows, b, width), jnp.float32)
    return pl.pallas_call(
        functools.partial(kernel, ncol, n, b, half, SYMMETRIC),
        out_shape=(out, out),
        in_specs=[pl.BlockSpec(memory_space=pl.ANY)] * 3
        + [pl.BlockSpec(memory_space=pltpu.SMEM)],
        out_specs=[pl.BlockSpec(memory_space=pltpu.VMEM)] * 2,
        scratch_shapes=[
            wide, wide, wide, row, row, row, row, row,
            row, pltpu.VMEM((3, band, b, b), bf), row, row, row, row,
            pltpu.VMEM((8, 128), bf),
            pltpu.SemaphoreType.DMA((3,)),
            pltpu.SemaphoreType.DMA((3, 13)),
            pltpu.SemaphoreType.DMA((3, 13)),
            pltpu.SemaphoreType.DMA((3, 2 * half)),
            pltpu.SemaphoreType.DMA((3, 2 * half)),
        ],
        compiler_params=pltpu.CompilerParams(
            collective_id=0, has_side_effects=True, vmem_limit_bytes=48 * 1024 * 1024),
        name="density_step",
    )(margin, fock_matrix, density, present)


def solution(mesh):
    nrow, ncol = mesh.shape["row"], mesh.shape["col"]
    spec3 = P(("row", "col"), None, None)
    return jax.shard_map(
        functools.partial(local, ncol, nrow * ncol), mesh=mesh,
        in_specs=(spec3, spec3, spec3, P(("row", "col"), None)),
        out_specs=(spec3, spec3), check_vma=False)
```

time: 242 us -> 81.4 us (0.34)
  the two profiles are of different devices: /device:TPU:10 before, /device:TPU:16 now
where the time goes in v1:
time: 81.4 us; the launch traced here: 81.2 us
  Pallas kernels  75.4 us (93%)
  local copies, waits for them, and re-layouts  5.16 us (6%)
    pallas_call x1, Pallas kernels, local(): pl.pallas_call(functools.partial(kernel, ncol, n, b, half, SYMMETRIC), ou...  75.4 us
    unnamed x10, local copies, waits for them, and re-layouts  5.16 us

profile of v1, /device:TPU:16, one launch (start us, length us, event | category | flops | bytes accessed | tf_op | source)
XLA Modules:
  0.0 81.2 jit_solution(4835132541791055186)
XLA Ops:
  0.6 0.0 copy-start
  0.6 1.0 %copy-done = bf16[1,128,1152]{2,1,0:T(8,128)(2,1)S(1)} copy-done((bf16[1,128,1152]{2,1,0:T(8,128)(2,1)S(1)}, bf16[1,128,1152]{2,1,0:T(8,128)(2,1)}, u32[]{:S(2)}) %copy-start) | copy-done | bytes 294936
  1.6 0.0 copy-start.1
  1.6 1.0 %copy-done.1 = bf16[1,128,1152]{2,1,0:T(8,128)(2,1)S(1)} copy-done((bf16[1,128,1152]{2,1,0:T(8,128)(2,1)S(1)}, bf16[1,128,1152]{2,1,0:T(8,128)(2,1)}, u32[]{:S(2)}) %copy-start.1) | copy-done | bytes 294936
  2.6 0.0 copy-start.2
  2.6 1.0 %copy-done.2 = bf16[1,128,1152]{2,1,0:T(8,128)(2,1)S(1)} copy-done((bf16[1,128,1152]{2,1,0:T(8,128)(2,1)S(1)}, bf16[1,128,1152]{2,1,0:T(8,128)(2,1)}, u32[]{:S(2)}) %copy-start.2) | copy-done | bytes 294936
  3.5 0.0 copy-start.3
  3.5 0.7 copy-done.3
  4.2 75.4 %density_step.1 = (f32[1,128,1152]{2,1,0:T(8,128)S(1)}, f32[1,128,1152]{2,1,0:T(8,128)S(1)}) custom-call(bf16[1,128,1152]{2,1,0:T(8,128)(2,1)S(1)} %copy-done, bf16[1,128,1152]{2,1,0:T(8,128)(2,1)S(1)} %copy-done.1, bf16[1,128,1152]{2,1,0:T(8,128)(2,1)S(1)} %copy-done.2, s32[1,9]{1,0:T(1,128)S(1)} %copy-done.3), custom_call_target="tpu_custom_call" | custom-call | tf_op jit(solution)/shard_map/density_step/pallas_call | solution.py:196
  79.5 0.8 %copy.8 = f32[1,128,1152]{2,1,0:T(8,128)} copy(f32[1,128,1152]{2,1,0:T(8,128)S(1)} %get-tuple-element.4) | data formatting | bytes 1179648
  80.4 0.8 %copy.9 = f32[1,128,1152]{2,1,0:T(8,128)} copy(f32[1,128,1152]{2,1,0:T(8,128)S(1)} %get-tuple-element.5) | data formatting | bytes 1179648
Async XLA Ops:
  0.6 1.0 %copy-start = (bf16[1,128,1152]{2,1,0:T(8,128)(2,1)S(1)}, bf16[1,128,1152]{2,1,0:T(8,128)(2,1)}, u32[]{:S(2)}) copy-start(bf16[1,128,1152]{2,1,0:T(8,128)(2,1)} %margin.1) | copy-start | bytes 884740
  1.6 1.0 %copy-start.1 = (bf16[1,128,1152]{2,1,0:T(8,128)(2,1)S(1)}, bf16[1,128,1152]{2,1,0:T(8,128)(2,1)}, u32[]{:S(2)}) copy-start(bf16[1,128,1152]{2,1,0:T(8,128)(2,1)} %fock.1) | copy-start | bytes 884740
  2.6 1.0 %copy-start.2 = (bf16[1,128,1152]{2,1,0:T(8,128)(2,1)S(1)}, bf16[1,128,1152]{2,1,0:T(8,128)(2,1)}, u32[]{:S(2)}) copy-start(bf16[1,128,1152]{2,1,0:T(8,128)(2,1)} %density.1) | copy-start | bytes 884740
  3.5 0.7 copy-start.3

commit v2 on v1

--- a/solution.py
+++ b/solution.py
@@ -8,11 +8,10 @@
 from jax.sharding import PartitionSpec as P
 
 STEP_SCALE = 0.015625
-SYMMETRIC = False
-
-
-def kernel(ncol, n, b, half, sym, margin, fock, density, present, grad, upd,
-           sw, xw, tw, xrow, trow, dv, fv, mv, gd, gm, cf, ch, co, qd, qm,
+
+
+def kernel(ncol, n, b, half, margin, fock, density, kept, grad, upd,
+           sw, xw, tw, xrow, trow, dv, fv, mv, gd, gm, cf, cm, ch, co, qd, present,
            lsem, wsend, wrecv, msend, mrecv):
     band = 2 * half + 1
     r = lax.axis_index("row") * ncol + lax.axis_index("col")
@@ -41,6 +40,7 @@
         pltpu.make_async_copy(margin.at[0], mv, lsem.at[0]),
         pltpu.make_async_copy(density.at[0], dv, lsem.at[1]),
         pltpu.make_async_copy(fock.at[0], fv, lsem.at[2]),
+        pltpu.make_async_copy(kept, present, lsem.at[3]),
     ]
     for c in loads:
         c.start()
@@ -61,7 +61,7 @@
     for d in offsets:
         @pl.when(jnp.logical_not(valid(-d)))
         def _():
-            for m in (gm.at[0], gm.at[1], gm.at[2]):
+            for m in (gm.at[0], gm.at[1]):
                 m[half - d] = jnp.zeros((b, b), gm.dtype)
 
     expected = jnp.minimum(r, half) + jnp.minimum(n - 1 - r, half)
@@ -72,25 +72,54 @@
     def window_plan(symmetric):
         plan = []
         for e in hops:
-            if e > 0:
-                s0 = 2 * e - 1
-                plan.append((e, s0, band - s0, core - 1))
+            m = abs(e)
+            if symmetric:
+                near = half - 2 * m + 2
+                if e > 0:
+                    plan.append((e, 2 * m - core, near, 0))
+                    if 4 * m - 1 <= half:
+                        plan.append((e, band - 2, 2, half + 1 + core))
+                else:
+                    plan.append((e, half - core, near, half + 2 * m))
+            elif e > 0:
+                plan.append((e, 2 * m - 1, band - 2 * m + 1, core - 1))
             else:
-                plan.append((e, 0, band + 2 * e + 1, core - 2 * e))
+                plan.append((e, 0, band - 2 * m + 1, core + 2 * m))
         return plan
 
-    def spread(phase, own, w, symmetric):
-        plan = window_plan(symmetric)
+    def known_blocks():
+        known = set()
+        for m in range(1, reach + 1):
+            for c in (0, 1):
+                known |= {(half - 2 * m + c, j) for j in range(half - 2 * m + 2)}
+                known |= {(half + 2 * m + c, j) for j in range(half + 2 * m, band + 1)}
+                if 4 * m - 1 <= half:
+                    known |= {(half - 2 * m + c, half + 1 + c + j) for j in (0, 1)}
+        return known
+
+    def reflect(w, sign, own_rows):
+        known = known_blocks()
+        middle = (half, half + 1)
+        for i in range(band + 1):
+            for j in range(band + 1):
+                if abs(i - j) > half or i in middle or (i, j) in known:
+                    continue
+                if (j in middle) != own_rows:
+                    continue
+                block = w[j * b:(j + 1) * b, (i + 1) * b:(i + 2) * b].T
+                w[i * b:(i + 1) * b, (j + 1) * b:(j + 2) * b] = block if sign > 0 else -block
+
+    def spread(phase, own, w, sign, beside=None):
+        plan = window_plan(sign != 0)
         here = pl.ds(pl.multiple_of((half + core) * b, b), b)
         copies = []
         for i, (e, s0, count, c0) in enumerate(plan):
             p = half - 2 * e + core
             spot = w.at[pl.ds(pl.multiple_of(p * b, b), b), col(c0 + 1, count)]
-            src = own.at[:, s0 * b:(s0 + count) * b]
             send = pltpu.make_async_remote_copy(
-                src_ref=src, dst_ref=spot, send_sem=wsend.at[phase, i],
-                recv_sem=wrecv.at[phase, i], device_id=device(r + 2 * e),
-                device_id_type=pl.DeviceIdType.MESH)
+                src_ref=own.at[:, col(s0, count)], dst_ref=spot,
+                send_sem=wsend.at[phase, i], recv_sem=wrecv.at[phase, i],
+                device_id=device(r + 2 * e), device_id_type=pl.DeviceIdType.MESH)
             relay = pltpu.make_async_remote_copy(
                 src_ref=spot, dst_ref=spot, send_sem=wsend.at[phase, 6 + i],
                 recv_sem=wrecv.at[phase, 6 + i], device_id=sibling,
@@ -106,12 +135,18 @@
             device_id=sibling, device_id_type=pl.DeviceIdType.MESH)
         share.start()
         w[here, col(core + 1, band)] = own[...]
+        if sign:
+            share.wait_recv()
+            reflect(w, sign, True)
+        if beside is not None:
+            beside()
         for e, send, relay in copies:
             @pl.when(valid_chip(-e))
             def _():
                 send.wait_recv()
                 relay.start()
-        share.wait_recv()
+        if not sign:
+            share.wait_recv()
         for e, send, relay in copies:
             @pl.when(valid_chip(-e))
             def _():
@@ -119,6 +154,8 @@
             pending.append((valid_chip(e), send))
             pending.append((valid_chip(-e), relay))
         pending.append((None, share))
+        if sign:
+            reflect(w, sign, False)
 
     def mirror(phase, own, m):
         copies = []
@@ -148,11 +185,21 @@
             keep = present[0, c].astype(jnp.float32)
             out[:, c * b:(c + 1) * b] = (acc * keep).astype(out.dtype)
 
+    def transposed_first():
+        for c in range(band):
+            lo, hi = max(0, c - half), min(band, c + half + 1)
+            rhs = xw[pl.ds(pl.multiple_of((core + c) * b, b), b), col(core + 1 + lo, hi - lo)]
+            acc = lax.dot_general(trow[:, lo * b:hi * b], rhs, (((1,), (1,)), ((), ())),
+                                  preferred_element_type=jnp.float32)
+            keep = present[0, c].astype(jnp.float32)
+            cm[:, c * b:(c + 1) * b] = (acc * -keep).astype(cm.dtype)
+
     loads[0].wait()
-    spread(0, mv, sw, sym)
+    spread(0, mv, sw, 1)
     loads[1].wait()
+    loads[3].wait()
     product(dv, sw, xrow)
-    spread(1, xrow, xw, False)
+    spread(1, xrow, xw, 0)
     loads[2].wait()
     product(fv, xw, gd)
     mirror(0, gd, gm.at[0])
@@ -161,20 +208,17 @@
         g = gd[:, cols].astype(jnp.float32) - gm[0, c].T.astype(jnp.float32)
         grad[0, :, cols] = g
         trow[:, cols] = (-STEP_SCALE * g).astype(trow.dtype)
-    spread(2, trow, tw, sym)
+    spread(2, trow, tw, -1, transposed_first)
     product(xrow, tw, cf)
-    mirror(1, cf, gm.at[1])
+    v = cf[...].astype(jnp.float32) + cm[...].astype(jnp.float32)
+    upd[0] = dv[...].astype(jnp.float32) + v
+    ch[...] = v.astype(ch.dtype)
+    product(ch, sw, co)
+    product(co, tw, qd)
+    mirror(1, qd, gm.at[1])
     for c in range(band):
         cols = slice(c * b, (c + 1) * b)
-        v = cf[:, cols].astype(jnp.float32) + gm[1, c].T.astype(jnp.float32)
-        upd[0, :, cols] = dv[:, cols].astype(jnp.float32) + v
-        ch[:, cols] = v.astype(ch.dtype)
-    product(ch, sw, co)
-    product(co, tw, qd)
-    mirror(2, qd, gm.at[2])
-    for c in range(band):
-        cols = slice(c * b, (c + 1) * b)
-        q = qd[:, cols].astype(jnp.float32) + gm[2, c].T.astype(jnp.float32)
+        q = qd[:, cols].astype(jnp.float32) + gm[1, c].T.astype(jnp.float32)
         upd[0, :, cols] += 0.5 * q
     for cond, c in pending:
         if cond is None:
@@ -194,23 +238,22 @@
     wide = pltpu.VMEM(((band + 1) * b, (band + 3) * b), bf)
     out = jax.ShapeDtypeStruct((rows, b, width), jnp.float32)
     return pl.pallas_call(
-        functools.partial(kernel, ncol, n, b, half, SYMMETRIC),
+        functools.partial(kernel, ncol, n, b, half),
         out_shape=(out, out),
-        in_specs=[pl.BlockSpec(memory_space=pl.ANY)] * 3
-        + [pl.BlockSpec(memory_space=pltpu.SMEM)],
+        in_specs=[pl.BlockSpec(memory_space=pl.ANY)] * 4,
         out_specs=[pl.BlockSpec(memory_space=pltpu.VMEM)] * 2,
         scratch_shapes=[
             wide, wide, wide, row, row, row, row, row,
-            row, pltpu.VMEM((3, band, b, b), bf), row, row, row, row,
-            pltpu.VMEM((8, 128), bf),
-            pltpu.SemaphoreType.DMA((3,)),
+            row, pltpu.VMEM((2, band, b, b), bf), row, row, row, row, row,
+            pltpu.SMEM((rows, band), jnp.int32),
+            pltpu.SemaphoreType.DMA((4,)),
             pltpu.SemaphoreType.DMA((3, 13)),
             pltpu.SemaphoreType.DMA((3, 13)),
-            pltpu.SemaphoreType.DMA((3, 2 * half)),
-            pltpu.SemaphoreType.DMA((3, 2 * half)),
+            pltpu.SemaphoreType.DMA((2, 2 * half)),
+            pltpu.SemaphoreType.DMA((2, 2 * half)),
         ],
         compiler_params=pltpu.CompilerParams(
-            collective_id=0, has_side_effects=True, vmem_limit_bytes=48 * 1024 * 1024),
+            collective_id=0, has_side_effects=True, vmem_limit_bytes=67043328),
         name="density_step",
     )(margin, fock_matrix, density, present)
 

time: 81.4 us -> 60.4 us (0.74)
  the two profiles are of different devices: /device:TPU:16 before, /device:TPU:10 now
where the time goes in v2:
time: 60.4 us; the launch traced here: 60.3 us
  Pallas kernels  56.8 us (94%)
  local copies, waits for them, and re-layouts  2.8 us (5%)
  between operations  0.65 us (1%)
    pallas_call x1, Pallas kernels, local(): pl.pallas_call(functools.partial(kernel, ncol, n, b, half), out_shape=(ou...  56.8 us
    unnamed x4, local copies, waits for them, and re-layouts  2.8 us

profile of v2, /device:TPU:10, one launch (start us, length us, event | category | flops | bytes accessed | tf_op | source)
XLA Modules:
  0.0 60.3 jit_solution(3900958220912541417)
XLA Ops:
  0.6 56.8 %density_step.1 = (f32[1,128,1152]{2,1,0:T(8,128)}, f32[1,128,1152]{2,1,0:T(8,128)}) custom-call(bf16[1,128,1152]{2,1,0:T(8,128)(2,1)} %margin.1, bf16[1,128,1152]{2,1,0:T(8,128)(2,1)} %fock.1, bf16[1,128,1152]{2,1,0:T(8,128)(2,1)} %density.1, s32[1,9]{1,0:T(1,128)} %kept.1), custom_call_target="tpu_custom_call" | custom-call | tf_op jit(solution)/shard_map/density_step/pallas_call | solution.py:240
  57.5 0.0 copy-start
  57.5 2.0 %copy.8 = f32[1,128,1152]{2,1,0:T(8,128)} copy(f32[1,128,1152]{2,1,0:T(8,128)} %get-tuple-element.4) | data formatting | bytes 1179648
  59.5 0.0 copy-done
  59.5 0.8 %copy.9 = f32[1,128,1152]{2,1,0:T(8,128)} copy(f32[1,128,1152]{2,1,0:T(8,128)S(1)} %copy-done) | data formatting | bytes 1179648
Async XLA Ops:
  57.5 2.0 %copy-start = (f32[1,128,1152]{2,1,0:T(8,128)S(1)}, f32[1,128,1152]{2,1,0:T(8,128)}, u32[]{:S(2)}) copy-start(f32[1,128,1152]{2,1,0:T(8,128)} %get-tuple-element.5) | copy-start | bytes 1769476

commit v3 on v2

--- a/solution.py
+++ b/solution.py
@@ -69,33 +69,27 @@
 
     pending = []
 
-    def window_plan(symmetric):
+    def window_plan(symmetric, c):
         plan = []
         for e in hops:
             m = abs(e)
-            if symmetric:
-                near = half - 2 * m + 2
-                if e > 0:
-                    plan.append((e, 2 * m - core, near, 0))
-                    if 4 * m - 1 <= half:
-                        plan.append((e, band - 2, 2, half + 1 + core))
-                else:
-                    plan.append((e, half - core, near, half + 2 * m))
+            p = half - 2 * e + c
+            if not symmetric:
+                lo, hi = max(0, p - half), min(band, p + half)
+                plan.append((e, p, lo, hi - lo + 1))
             elif e > 0:
-                plan.append((e, 2 * m - 1, band - 2 * m + 1, core - 1))
+                plan.append((e, p, 0, p + 1))
+                if m == 1 and c == 1:
+                    plan.append((e, p, half + 2, 2))
             else:
-                plan.append((e, 0, band - 2 * m + 1, core + 2 * m))
+                plan.append((e, p, p, band + 1 - p))
+                if m == 1 and c == 0:
+                    plan.append((e, p, half - 2, 1))
         return plan
 
     def known_blocks():
-        known = set()
-        for m in range(1, reach + 1):
-            for c in (0, 1):
-                known |= {(half - 2 * m + c, j) for j in range(half - 2 * m + 2)}
-                known |= {(half + 2 * m + c, j) for j in range(half + 2 * m, band + 1)}
-                if 4 * m - 1 <= half:
-                    known |= {(half - 2 * m + c, half + 1 + c + j) for j in (0, 1)}
-        return known
+        return {(p, j) for c in (0, 1) for _, p, lo, count in window_plan(True, c)
+                for j in range(lo, lo + count)}
 
     def reflect(w, sign, own_rows):
         known = known_blocks()
@@ -109,26 +103,34 @@
                 block = w[j * b:(j + 1) * b, (i + 1) * b:(i + 2) * b].T
                 w[i * b:(i + 1) * b, (j + 1) * b:(j + 2) * b] = block if sign > 0 else -block
 
+    def both(x, y):
+        return jnp.logical_and(x, y)
+
     def spread(phase, own, w, sign, beside=None):
-        plan = window_plan(sign != 0)
         here = pl.ds(pl.multiple_of((half + core) * b, b), b)
-        copies = []
-        for i, (e, s0, count, c0) in enumerate(plan):
-            p = half - 2 * e + core
-            spot = w.at[pl.ds(pl.multiple_of(p * b, b), b), col(c0 + 1, count)]
-            send = pltpu.make_async_remote_copy(
-                src_ref=own.at[:, col(s0, count)], dst_ref=spot,
-                send_sem=wsend.at[phase, i], recv_sem=wrecv.at[phase, i],
-                device_id=device(r + 2 * e), device_id_type=pl.DeviceIdType.MESH)
-            relay = pltpu.make_async_remote_copy(
-                src_ref=spot, dst_ref=spot, send_sem=wsend.at[phase, 6 + i],
-                recv_sem=wrecv.at[phase, 6 + i], device_id=sibling,
-                device_id_type=pl.DeviceIdType.MESH)
-
-            @pl.when(valid_chip(e))
-            def _():
-                send.start()
-            copies.append((e, send, relay))
+        sends, relays = [], []
+        for cc in (0, 1):
+            mine, theirs = core == cc, core == 1 - cc
+            for i, (e, p, lo, count) in enumerate(window_plan(sign != 0, cc)):
+                spot = w.at[p * b:(p + 1) * b, (lo + 1) * b:(lo + 1 + count) * b]
+                s0 = lo - p + half
+                send = pltpu.make_async_remote_copy(
+                    src_ref=own.at[:, s0 * b:(s0 + count) * b], dst_ref=spot,
+                    send_sem=wsend.at[phase, i], recv_sem=wrecv.at[phase, i],
+                    device_id=device(r + 2 * e), device_id_type=pl.DeviceIdType.MESH)
+                out, back = both(mine, valid_chip(e)), both(mine, valid_chip(-e))
+                relay = None
+                if 0 < p < band:
+                    relay = pltpu.make_async_remote_copy(
+                        src_ref=spot, dst_ref=spot, send_sem=wsend.at[phase, 6 + i],
+                        recv_sem=wrecv.at[phase, 6 + i], device_id=sibling,
+                        device_id_type=pl.DeviceIdType.MESH)
+                    relays.append((relay, back, both(theirs, valid_chip(-e))))
+
+                @pl.when(out)
+                def _():
+                    send.start()
+                sends.append((send, relay, out, back))
         share = pltpu.make_async_remote_copy(
             src_ref=own, dst_ref=w.at[here, col(core + 1, band)],
             send_sem=wsend.at[phase, 12], recv_sem=wrecv.at[phase, 12],
@@ -140,19 +142,20 @@
             reflect(w, sign, True)
         if beside is not None:
             beside()
-        for e, send, relay in copies:
-            @pl.when(valid_chip(-e))
+        for send, relay, out, back in sends:
+            @pl.when(back)
             def _():
                 send.wait_recv()
-                relay.start()
+                if relay is not None:
+                    relay.start()
+            pending.append((out, send))
         if not sign:
             share.wait_recv()
-        for e, send, relay in copies:
-            @pl.when(valid_chip(-e))
+        for relay, started, arriving in relays:
+            @pl.when(arriving)
             def _():
                 relay.wait_recv()
-            pending.append((valid_chip(e), send))
-            pending.append((valid_chip(-e), relay))
+            pending.append((started, relay))
         pending.append((None, share))
         if sign:
             reflect(w, sign, False)
@@ -240,7 +243,7 @@
     return pl.pallas_call(
         functools.partial(kernel, ncol, n, b, half),
         out_shape=(out, out),
-        in_specs=[pl.BlockSpec(memory_space=pl.ANY)] * 4,
+        in_specs=[pl.BlockSpec(memory_space=pltpu.HBM)] * 4,
         out_specs=[pl.BlockSpec(memory_space=pltpu.VMEM)] * 2,
         scratch_shapes=[
             wide, wide, wide, row, row, row, row, row,
@@ -253,7 +256,7 @@
             pltpu.SemaphoreType.DMA((2, 2 * half)),
         ],
         compiler_params=pltpu.CompilerParams(
-            collective_id=0, has_side_effects=True, vmem_limit_bytes=67043328),
+            collective_id=0, has_side_effects=True, vmem_limit_bytes=48 * 1024 * 1024),
         name="density_step",
     )(margin, fock_matrix, density, present)
 

time: 60.4 us -> 57.8 us (0.957)
  Pallas kernels: 56.8 us -> 51.5 us
  local copies, waits for them, and re-layouts: 2.8 us -> 5.16 us
    pallas_call x1, Pallas kernels: 56.8 us -> 51.5 us  [local(): pl.pallas_call(functools.partial(kernel, ncol, n, b, half), out_shape=(ou...]
    unnamed x4 -> x10, local copies, waits for them, and re-layouts: 2.8 us -> 5.16 us
where the time goes in v3:
time: 57.8 us; the launch traced here: 57.3 us
  Pallas kernels  51.5 us (89%)
  local copies, waits for them, and re-layouts  5.16 us (9%)
  between operations  0.65 us (1%)
    pallas_call x1, Pallas kernels, local(): pl.pallas_call(functools.partial(kernel, ncol, n, b, half), out_shape=(ou...  51.5 us
    unnamed x10, local copies, waits for them, and re-layouts  5.16 us

profile of v3, /device:TPU:10, one launch (start us, length us, event | category | flops | bytes accessed | tf_op | source)
XLA Modules:
  0.0 57.3 jit_solution(14145122955001133725)
XLA Ops:
  0.6 0.0 copy-start
  0.6 1.0 %copy-done = bf16[1,128,1152]{2,1,0:T(8,128)(2,1)S(1)} copy-done((bf16[1,128,1152]{2,1,0:T(8,128)(2,1)S(1)}, bf16[1,128,1152]{2,1,0:T(8,128)(2,1)}, u32[]{:S(2)}) %copy-start) | copy-done | bytes 294936
  1.6 0.0 copy-start.1
  1.6 1.0 %copy-done.1 = bf16[1,128,1152]{2,1,0:T(8,128)(2,1)S(1)} copy-done((bf16[1,128,1152]{2,1,0:T(8,128)(2,1)S(1)}, bf16[1,128,1152]{2,1,0:T(8,128)(2,1)}, u32[]{:S(2)}) %copy-start.1) | copy-done | bytes 294936
  2.6 0.0 copy-start.2
  2.6 1.0 %copy-done.2 = bf16[1,128,1152]{2,1,0:T(8,128)(2,1)S(1)} copy-done((bf16[1,128,1152]{2,1,0:T(8,128)(2,1)S(1)}, bf16[1,128,1152]{2,1,0:T(8,128)(2,1)}, u32[]{:S(2)}) %copy-start.2) | copy-done | bytes 294936
  3.5 0.0 copy-start.3
  3.5 0.7 %copy-done.3 = s32[1,9]{1,0:T(1,128)S(1)} copy-done((s32[1,9]{1,0:T(1,128)S(1)}, s32[1,9]{1,0:T(1,128)}, u32[]{:S(2)}) %copy-start.3) | copy-done | bytes 60
  4.2 51.5 %density_step.1 = (f32[1,128,1152]{2,1,0:T(8,128)S(1)}, f32[1,128,1152]{2,1,0:T(8,128)S(1)}) custom-call(bf16[1,128,1152]{2,1,0:T(8,128)(2,1)S(1)} %copy-done, bf16[1,128,1152]{2,1,0:T(8,128)(2,1)S(1)} %copy-done.1, bf16[1,128,1152]{2,1,0:T(8,128)(2,1)S(1)} %copy-done.2, s32[1,9]{1,0:T(1,128)S(1)} %copy-done.3), custom_call_target="tpu_custom_call" | custom-call | tf_op jit(solution)/shard_map/density_step/pallas_call | solution.py:243
  55.7 0.8 %copy.8 = f32[1,128,1152]{2,1,0:T(8,128)} copy(f32[1,128,1152]{2,1,0:T(8,128)S(1)} %get-tuple-element.4) | data formatting | bytes 1179648
  56.5 0.8 %copy.9 = f32[1,128,1152]{2,1,0:T(8,128)} copy(f32[1,128,1152]{2,1,0:T(8,128)S(1)} %get-tuple-element.5) | data formatting | bytes 1179648
Async XLA Ops:
  0.6 1.0 %copy-start = (bf16[1,128,1152]{2,1,0:T(8,128)(2,1)S(1)}, bf16[1,128,1152]{2,1,0:T(8,128)(2,1)}, u32[]{:S(2)}) copy-start(bf16[1,128,1152]{2,1,0:T(8,128)(2,1)} %margin.1) | copy-start | bytes 884740
  1.6 1.0 %copy-start.1 = (bf16[1,128,1152]{2,1,0:T(8,128)(2,1)S(1)}, bf16[1,128,1152]{2,1,0:T(8,128)(2,1)}, u32[]{:S(2)}) copy-start(bf16[1,128,1152]{2,1,0:T(8,128)(2,1)} %fock.1) | copy-start | bytes 884740
  2.6 1.0 %copy-start.2 = (bf16[1,128,1152]{2,1,0:T(8,128)(2,1)S(1)}, bf16[1,128,1152]{2,1,0:T(8,128)(2,1)}, u32[]{:S(2)}) copy-start(bf16[1,128,1152]{2,1,0:T(8,128)(2,1)} %density.1) | copy-start | bytes 884740
  3.5 0.7 %copy-start.3 = (s32[1,9]{1,0:T(1,128)S(1)}, s32[1,9]{1,0:T(1,128)}, u32[]{:S(2)}) copy-start(s32[1,9]{1,0:T(1,128)} %kept.1) | copy-start | bytes 112

commit v4 on v3

--- a/solution.py
+++ b/solution.py
@@ -10,9 +10,10 @@
 STEP_SCALE = 0.015625
 
 
-def kernel(ncol, n, b, half, margin, fock, density, kept, grad, upd,
-           sw, xw, tw, xrow, trow, dv, fv, mv, gd, gm, cf, cm, ch, co, qd, present,
-           lsem, wsend, wrecv, msend, mrecv):
+def kernel(ncol, n, b, half, margin, fock, density, kept, *rest):
+    outs, rest = rest[:6], rest[6:]
+    (sw, xw, tw, xrow, trow, dv, fv, mv, gd, gt, gm, cf, cm, ch, co, qd, qt, present,
+     lsem, osem, wsend, wrecv, msend, mrecv) = rest
     band = 2 * half + 1
     r = lax.axis_index("row") * ncol + lax.axis_index("col")
     k = r // 2
@@ -197,6 +198,14 @@
             keep = present[0, c].astype(jnp.float32)
             cm[:, c * b:(c + 1) * b] = (acc * -keep).astype(cm.dtype)
 
+    stores = []
+
+    def store(src):
+        i = len(stores)
+        c = pltpu.make_async_copy(src, outs[i].at[0], osem.at[i])
+        c.start()
+        stores.append(c)
+
     loads[0].wait()
     spread(0, mv, sw, 1)
     loads[1].wait()
@@ -205,24 +214,30 @@
     spread(1, xrow, xw, 0)
     loads[2].wait()
     product(fv, xw, gd)
+    store(gd)
     mirror(0, gd, gm.at[0])
     for c in range(band):
         cols = slice(c * b, (c + 1) * b)
-        g = gd[:, cols].astype(jnp.float32) - gm[0, c].T.astype(jnp.float32)
-        grad[0, :, cols] = g
+        other = gm[0, c].T
+        gt[:, cols] = other
+        g = gd[:, cols].astype(jnp.float32) - other.astype(jnp.float32)
         trow[:, cols] = (-STEP_SCALE * g).astype(trow.dtype)
+    store(gt)
     spread(2, trow, tw, -1, transposed_first)
     product(xrow, tw, cf)
+    store(cf)
+    store(cm)
     v = cf[...].astype(jnp.float32) + cm[...].astype(jnp.float32)
-    upd[0] = dv[...].astype(jnp.float32) + v
     ch[...] = v.astype(ch.dtype)
     product(ch, sw, co)
     product(co, tw, qd)
+    store(qd)
     mirror(1, qd, gm.at[1])
     for c in range(band):
-        cols = slice(c * b, (c + 1) * b)
-        q = qd[:, cols].astype(jnp.float32) + gm[1, c].T.astype(jnp.float32)
-        upd[0, :, cols] += 0.5 * q
+        qt[:, c * b:(c + 1) * b] = gm[1, c].T
+    store(qt)
+    for c in stores:
+        c.wait()
     for cond, c in pending:
         if cond is None:
             c.wait_send()
@@ -239,26 +254,29 @@
     bf = jnp.bfloat16
     row = pltpu.VMEM((b, width), bf)
     wide = pltpu.VMEM(((band + 1) * b, (band + 3) * b), bf)
-    out = jax.ShapeDtypeStruct((rows, b, width), jnp.float32)
-    return pl.pallas_call(
+    out = jax.ShapeDtypeStruct((rows, b, width), bf)
+    outs = pl.pallas_call(
         functools.partial(kernel, ncol, n, b, half),
-        out_shape=(out, out),
+        out_shape=(out,) * 6,
         in_specs=[pl.BlockSpec(memory_space=pltpu.HBM)] * 4,
-        out_specs=[pl.BlockSpec(memory_space=pltpu.VMEM)] * 2,
+        out_specs=[pl.BlockSpec(memory_space=pltpu.HBM)] * 6,
         scratch_shapes=[
             wide, wide, wide, row, row, row, row, row,
-            row, pltpu.VMEM((2, band, b, b), bf), row, row, row, row, row,
+            row, row, pltpu.VMEM((2, band, b, b), bf), row, row, row, row, row, row,
             pltpu.SMEM((rows, band), jnp.int32),
             pltpu.SemaphoreType.DMA((4,)),
+            pltpu.SemaphoreType.DMA((6,)),
             pltpu.SemaphoreType.DMA((3, 13)),
             pltpu.SemaphoreType.DMA((3, 13)),
             pltpu.SemaphoreType.DMA((2, 2 * half)),
             pltpu.SemaphoreType.DMA((2, 2 * half)),
         ],
         compiler_params=pltpu.CompilerParams(
-            collective_id=0, has_side_effects=True, vmem_limit_bytes=48 * 1024 * 1024),
+            collective_id=0, has_side_effects=True, vmem_limit_bytes=67043328),
         name="density_step",
     )(margin, fock_matrix, density, present)
+    gd, gt, cf, cm, qd, qt = (v.astype(jnp.float32) for v in outs)
+    return gd - gt, density.astype(jnp.float32) + (cf + cm) + 0.5 * (qd + qt)
 
 
 def solution(mesh):

time: 57.8 us -> 55.6 us (0.962)
  local copies, waits for them, and re-layouts: 5.16 us -> 0 us
  other arithmetic: 0 us -> 2.76 us
  Pallas kernels: 51.5 us -> 52.1 us
    unnamed x10 -> x0, local copies, waits for them, and re-layouts: 5.16 us -> none
    add x0 -> x1, other arithmetic: none -> 2.76 us  [local(): return (gd - gt, density.astype(jnp.float32) + (cf + cm) + 0.5 * (qd + qt))]
    pallas_call x1, Pallas kernels: 51.5 us -> 52.1 us  [local(): pl.pallas_call(functools.partial(kernel, ncol, n, b, half), out_shape=(ou...]
where the time goes in v4:
time: 55.6 us; the launch traced here: 55.5 us
  Pallas kernels  52.1 us (94%)
  other arithmetic  2.76 us (5%)
  between operations  0.64 us (1%)
    pallas_call x1, Pallas kernels, local(): pl.pallas_call(functools.partial(kernel, ncol, n, b, half), out_shape=(ou...  52.1 us
    add x1, other arithmetic, local(): return (gd - gt, density.astype(jnp.float32) + (cf + cm) + 0.5 * (qd + qt))  2.76 us

profile of v4, /device:TPU:10, one launch (start us, length us, event | category | flops | bytes accessed | tf_op | source)
XLA Modules:
  0.0 55.5 jit_solution(12088997702519500171)
XLA Ops:
  0.6 52.1 %density_step.1 = (bf16[1,128,1152]{2,1,0:T(8,128)(2,1)}, bf16[1,128,1152]{2,1,0:T(8,128)(2,1)}, bf16[1,128,1152]{2,1,0:T(8,128)(2,1)}, bf16[1,128,1152]{2,1,0:T...) custom-call(bf16[1,128,1152]{2,1,0:T(8,128)(2,1)} %margin.1, bf16[1,128,1152]{2,1,0:T(8,128)(2,1)} %fock.1, ...), custom_call_target="tpu_custom_call" | custom-call | tf_op jit(solution)/shard_map/density_step/pallas_call | solution.py:258
  52.7 2.8 %multiply_add_fusion = (f32[1,128,1152]{2,1,0:T(8,128)}, f32[1,128,1152]{2,1,0:T(8,128)}) fusion(bf16[1,128,1152]{2,1,0:T(8,128)(2,1)} %get-tuple-element.13, bf16[1,128,1152]{2,1,0:T(8,128)(2,1)} %get-tuple-element.12, bf16[1,128,1152]{2,1,0:T(8,128)(2,1)} %get-tuple-element.11, bf16[1,128,1152]{2,1,0:T(8,128)(2,1)} %get-tuple-element.10, ...), kind=kLoop, calls=%fused_computation | loop fusion | flops 1916928 | bytes 3244032 | tf_op jit(solution)/shard_map/add | solution.py:279

commit v5 on v4

--- a/solution.py
+++ b/solution.py
@@ -11,8 +11,8 @@
 
 
 def kernel(ncol, n, b, half, margin, fock, density, kept, *rest):
-    outs, rest = rest[:6], rest[6:]
-    (sw, xw, tw, xrow, trow, dv, fv, mv, gd, gt, gm, cf, cm, ch, co, qd, qt, present,
+    outs, rest = rest[:5], rest[5:]
+    (sw, xw, tw, xrow, trow, dv, fv, mv, gd, gt, gm, cf, cm, ch, co, qd, qt, base, present,
      lsem, osem, wsend, wrecv, msend, mrecv) = rest
     band = 2 * half + 1
     r = lax.axis_index("row") * ncol + lax.axis_index("col")
@@ -161,9 +161,11 @@
         if sign:
             reflect(w, sign, False)
 
-    def mirror(phase, own, m):
+    def mirror(phase, left, w, own, m):
+        product(left, w, own, (half,))
         copies = []
         for i, d in enumerate(sorted(offsets, key=lambda v: -abs(v))):
+            product(left, w, own, (half + d,))
             c = pltpu.make_async_remote_copy(
                 src_ref=own.at[:, (half + d) * b:(half + d + 1) * b],
                 dst_ref=m.at[half - d], send_sem=msend.at[phase, i],
@@ -181,8 +183,8 @@
                 c.wait_recv()
             pending.append((valid(d), c))
 
-    def product(left, w, out):
-        for c in range(band):
+    def product(left, w, out, columns=None):
+        for c in columns or range(band):
             lo, hi = max(0, c - half), min(band, c + half + 1)
             rhs = w[pl.ds(pl.multiple_of((core + lo) * b, b), (hi - lo) * b), col(core + 1 + c)]
             acc = jnp.dot(left[:, lo * b:hi * b], rhs, preferred_element_type=jnp.float32)
@@ -213,9 +215,8 @@
     product(dv, sw, xrow)
     spread(1, xrow, xw, 0)
     loads[2].wait()
-    product(fv, xw, gd)
+    mirror(0, fv, xw, gd, gm.at[0])
     store(gd)
-    mirror(0, gd, gm.at[0])
     for c in range(band):
         cols = slice(c * b, (c + 1) * b)
         other = gm[0, c].T
@@ -225,14 +226,13 @@
     store(gt)
     spread(2, trow, tw, -1, transposed_first)
     product(xrow, tw, cf)
-    store(cf)
-    store(cm)
     v = cf[...].astype(jnp.float32) + cm[...].astype(jnp.float32)
     ch[...] = v.astype(ch.dtype)
+    base[...] = dv[...].astype(jnp.float32) + v
+    store(base)
     product(ch, sw, co)
-    product(co, tw, qd)
+    mirror(1, co, tw, qd, gm.at[1])
     store(qd)
-    mirror(1, qd, gm.at[1])
     for c in range(band):
         qt[:, c * b:(c + 1) * b] = gm[1, c].T
     store(qt)
@@ -257,15 +257,15 @@
     out = jax.ShapeDtypeStruct((rows, b, width), bf)
     outs = pl.pallas_call(
         functools.partial(kernel, ncol, n, b, half),
-        out_shape=(out,) * 6,
+        out_shape=(out, out, jax.ShapeDtypeStruct((rows, b, width), jnp.float32), out, out),
         in_specs=[pl.BlockSpec(memory_space=pltpu.HBM)] * 4,
-        out_specs=[pl.BlockSpec(memory_space=pltpu.HBM)] * 6,
+        out_specs=[pl.BlockSpec(memory_space=pltpu.HBM)] * 5,
         scratch_shapes=[
             wide, wide, wide, row, row, row, row, row,
             row, row, pltpu.VMEM((2, band, b, b), bf), row, row, row, row, row, row,
-            pltpu.SMEM((rows, band), jnp.int32),
+            pltpu.VMEM((b, width), jnp.float32), pltpu.SMEM((rows, band), jnp.int32),
             pltpu.SemaphoreType.DMA((4,)),
-            pltpu.SemaphoreType.DMA((6,)),
+            pltpu.SemaphoreType.DMA((5,)),
             pltpu.SemaphoreType.DMA((3, 13)),
             pltpu.SemaphoreType.DMA((3, 13)),
             pltpu.SemaphoreType.DMA((2, 2 * half)),
@@ -275,8 +275,8 @@
             collective_id=0, has_side_effects=True, vmem_limit_bytes=67043328),
         name="density_step",
     )(margin, fock_matrix, density, present)
-    gd, gt, cf, cm, qd, qt = (v.astype(jnp.float32) for v in outs)
-    return gd - gt, density.astype(jnp.float32) + (cf + cm) + 0.5 * (qd + qt)
+    gd, gt, base, qd, qt = (v.astype(jnp.float32) for v in outs)
+    return gd - gt, base + 0.5 * (qd + qt)
 
 
 def solution(mesh):

time: 55.6 us -> 55.3 us (level)
  no operation moved by 1% of the time
where the time goes in v5:
time: 55.3 us; the launch traced here: 54.9 us
  Pallas kernels  51.7 us (93%)
  other arithmetic  2.57 us (5%)
  between operations  0.64 us (1%)
    pallas_call x1, Pallas kernels, local(): pl.pallas_call(functools.partial(kernel, ncol, n, b, half), out_shape=(ou...  51.7 us
    add x1, other arithmetic, local(): return (gd - gt, base + 0.5 * (qd + qt))  2.57 us

profile of v5, /device:TPU:10, one launch (start us, length us, event | category | flops | bytes accessed | tf_op | source)
XLA Modules:
  0.0 54.9 jit_solution(9798300085798066787)
XLA Ops:
  0.6 51.7 %density_step.1 = (bf16[1,128,1152]{2,1,0:T(8,128)(2,1)}, bf16[1,128,1152]{2,1,0:T(8,128)(2,1)}, f32[1,128,1152]{2,1,0:T(8,128)}, bf16[1,128,1152]{2,1,0:T(8,128)(2,1)}, bf16[1,128,1152]{2,1,0:T(8,128)(2,1)}) custom-call(bf16[1,128,1152]{2,1,0:T(8,128)(2,1)} %margin.1, bf16[1,128,1152]{2,1,0:T(8,128)(2,1)} %fock.1, bf16[1,128,1152]{2,1,0:T(8,128)(2,1)} %density.1, ...), custom_call_target="tpu_custom_call" | custom-call | tf_op jit(solution)/shard_map/density_step/pallas_call | solution.py:258
  52.4 2.6 %multiply_add_fusion = (f32[1,128,1152]{2,1,0:T(8,128)}, f32[1,128,1152]{2,1,0:T(8,128)}) fusion(f32[1,128,1152]{2,1,0:T(8,128)} %get-tuple-element.9, bf16[1,128,1152]{2,1,0:T(8,128)(2,1)} %get-tuple-element.11, bf16[1,128,1152]{2,1,0:T(8,128)(2,1)} %get-tuple-element.10, bf16[1,128,1152]{2,1,0:T(8,128)(2,1)} %get-tuple-element.8, ...), kind=kLoop, calls=%fused_computation | loop fusion | flops 1179648 | bytes 2949120 | tf_op jit(solution)/shard_map/add | solution.py:279
